TPU v7x, 128 devices: a whole 4x4x4 slice. The times are simulated.
128 devices in a mesh: region: 32 (over z, y, core), blk: 4 (over x).
Axes of the slice: x: 4, y: 4, z: 4, core: 2. Of those that a mesh axis runs over, the one named last changes fastest.
Arguments:
- jac_bus: float32 [1024, 8, 128, 128], P('region', 'blk'), may hold values from -0.1875 to 0.1875
- pattern: int32 [1024, 8], P(('region', 'blk')), may hold values from 0 to 23
- branch_weight: float32 [1024, 128], P(('region', 'blk')), may hold values from 0.2 to 5
- bus_diag: float32 [1024, 128], P(('region', 'blk')), may hold values from 0.3 to 3
- right_side: float32 [1024, 128], P(('region', 'blk')), may hold values from -8 to 8
Outputs:
- solution: float32 [1024, 128], P(('region', 'blk'))
- residual: float32 [1024, 128], P(('region', 'blk'))
Inputs may be any that keep to these rules, and one draw needn't show every extreme that they name: pattern values below 8 name the region before the branch tile's region, those from 16 the region after it, with regions closed into a loop.
All inputs are finite; a program needn't handle non-finite values.
Results may differ from a plain program's by a relative error of at most 0.0003.
Values sent between devices are 32-bit elements; how exact they have to be, the bound alone decides.
A program may use at most 64 MiB of HBM per device.

v0:
```python
import functools

import jax
import jax.numpy as jnp
from jax import lax
from jax.sharding import Mesh
from jax.sharding import PartitionSpec as P

ITERS = 12
REGION = ("region_0", "region_1", "region_2")
REGION_BLK = ("region_0", "region_1", "region_2", "blk")


def extended(array, sides, width):
    for axis, dim in sides:
        size, length = (lax.axis_size(axis), array.shape[dim])
        up = [(i, (i + 1) % size) for i in range(size)]
        down = [(j, i) for i, j in up]
        last = lax.slice_in_dim(array, length - width, length, axis=dim)
        leading = lax.slice_in_dim(array, 0, width, axis=dim)
        before = lax.ppermute(last, axis, up)
        after = lax.ppermute(leading, axis, down)
        array = jnp.concatenate([before, array, after], axis=dim)
    return array


def from_behind(array, axis, by):
    length = lax.axis_size(axis)
    return lax.ppermute(array, axis, [(i, (i + by) % length) for i in range(length)])


def sent_to_all(array, axis):
    copies = jnp.broadcast_to(array, (lax.axis_size(axis), *array.shape))
    return lax.all_to_all(copies, axis, split_axis=0, concat_axis=0, tiled=True)


def joined_along(tiles, dim):
    dims = list(tiles.shape[1:])
    dims[dim] *= tiles.shape[0]
    return jnp.moveaxis(tiles, 0, dim).reshape(dims)


def gather_directly(array, axis, dim):
    tiles = sent_to_all(array, axis)
    return joined_along(tiles, dim)


def taken_together(array, axis):
    return sent_to_all(array, axis).sum(axis=0)


def over_axes(array, axes):
    return functools.reduce(lax.psum, axes, array)


def neighbours(values):
    return extended(values[None], ((REGION, 0),), 1)


def route(lower, middle, upper):
    from_upper = from_behind(lower, REGION, -1)
    from_lower = from_behind(upper, REGION, 1)
    return middle + from_upper + from_lower


def spread(tiles, weight, index, count):
    back = jnp.einsum("tjab,ta->tjb", tiles, weight, precision=lax.Precision.HIGHEST)
    width = back.shape[-1]
    return jnp.zeros((count, width), jnp.float32).at[index.reshape(-1)].add(back.reshape(-1, width))


def body(jac_bus, pattern, branch_weight, bus_diag, right_side):
    hp = lax.Precision.HIGHEST
    per_dev = right_side.shape[0]
    width = right_side.shape[1]
    group_len = jac_bus.shape[1]
    member = lax.axis_index("blk")
    cols_all, weight = (
        gather_directly(pattern, "blk", 0),
        gather_directly(branch_weight, "blk", 0),
    )
    index = lax.dynamic_slice_in_dim(cols_all, member * group_len, group_len, 1)

    def collect(buffer):
        parts = buffer.reshape(3, per_dev, width)
        return route(parts[0], parts[1], parts[2])

    def branch_rows(vector):
        flat = neighbours(vector).reshape(-1, width)
        partial_value = jnp.einsum("tjab,tjb->ta", jac_bus, flat[index], precision=hp)
        return taken_together(partial_value, "blk")

    count = 3 * per_dev

    def apply_operator(vector):
        rows = branch_rows(vector)
        return bus_diag * vector + collect(spread(jac_bus, weight * rows, index, count))

    precond = bus_diag + collect(spread(jac_bus * jac_bus, weight, index, count))
    solution = jnp.zeros_like(right_side)
    residual = right_side

    def paired(resid):
        scaled = resid / precond
        image = apply_operator(scaled)
        gamma, delta = (
            over_axes(jnp.sum(resid * scaled), REGION_BLK),
            over_axes(jnp.sum(image * scaled), REGION_BLK),
        )
        return (scaled, image, gamma, delta)

    scaled, image, gamma, delta = paired(residual)
    alpha = gamma / delta
    direction, along = (scaled, image)
    solution = alpha * direction
    residual = residual - alpha * along

    def one_step(step, carry):
        solution, residual, direction, along, gamma, alpha = carry
        scaled, image, fresh, delta = paired(residual)
        beta = fresh / gamma
        alpha = fresh / (delta - beta * fresh / alpha)
        direction = scaled + beta * direction
        along = image + beta * along
        solution = solution + alpha * direction
        residual = residual - alpha * along
        return (solution, residual, direction, along, fresh, alpha)

    carry = lax.fori_loop(
        0, ITERS - 1, one_step, (solution, residual, direction, along, gamma, alpha)
    )
    solution, residual = (carry[0], carry[1])
    return (solution, residual)


def solution(mesh):
    finer = Mesh(
        mesh.devices.reshape(4, 4, 2, mesh.shape["blk"]),
        ("region_0", "region_1", "region_2", "blk"),
    )
    in_specs = (
        P(REGION, "blk", None, None),
        P(REGION_BLK, None),
        P(REGION_BLK, None),
        P(REGION_BLK, None),
        P(REGION_BLK, None),
    )
    out_specs = (P(REGION_BLK, None), P(REGION_BLK, None))
    return jax.shard_map(body, mesh=finer, in_specs=in_specs, out_specs=out_specs, check_vma=False)
```

profile of v0, /device:TPU:1, one launch (start us, length us, event | category | flops | bytes accessed | tf_op | source)
XLA Modules:
  0.0 856.5 jit_solution(12534373991295843344)
XLA Ops:
  2.0 4.8 all-to-all-start.1
  20.1 4.6 fusion.5
  33.2 5.5 collective-permute-start.7
  40.1 5.7 fusion.25
  45.8 6.8 all_to_all.21
  57.7 6.7 collective-permute-start.8
  69.6 6.7 all-reduce.6
  76.3 12.2 %all-reduce.5 = (f32[]{:T(128)}, f32[]{:T(128)}) all-reduce(f32[]{:T(128)} %get-tuple-element.107, f32[]{:T(128)} %get-tuple-element.108), channel_id=1, replica_groups=mesh['region_0'=4,'region_1'=4,'region_2'=2,'blk'=4] {'region_1'}, use_global_device_ids=true, to_apply=%region_3.0 | all-reduce | flops 2 | bytes 16 | tf_op jit(solution)/shard_map/psum | solution.py:53
  88.4 6.4 all-reduce.7
  94.9 7.7 all-reduce.4
  103.9 752.0 %while.20 = (s32[]{:T(128)}, f32[8,128]{1,0:T(8,128)S(1)}, f32[8,128]{1,0:T(8,128)S(1)}, f32[8,128]{1,0:T(8,128)S(1)}, f32[8,128]{1,0:T(8,128)S(1)}, /*index=5*/...) while((s32[]{:T(128)}, f32[8,128]{1,0:T(8,128)S(1)}, ...), condition=%wide.region_26.0_spmd, body=%wide.region_13.0_spmd.sunk | while | flops 25215368 | bytes 9170913 | solution.py:129
  109.8 5.7 fusion.51
  119.5 4.4 all-to-all-done
  136.5 7.7 all-reduce.12
  144.2 16.0 %all-reduce.13 = (f32[]{:T(128)}, f32[]{:T(128)}) all-reduce(f32[]{:T(128)} %get-tuple-element.225, f32[]{:T(128)} %get-tuple-element.226), channel_id=1, replica_groups=mesh['region_0'=4,'region_1'=4,'region_2'=2,'blk'=4] {'region_1'}, use_global_device_ids=true, to_apply=%region_16.0 | all-reduce | flops 2 | bytes 16 | tf_op jit(solution)/shard_map/while/body/eval_jaxpr/psum | solution.py:53
  163.4 7.5 all-reduce.15
  177.6 5.7 fusion.51
  187.2 4.4 all-to-all-done
  204.7 7.2 all-reduce.12
  211.9 16.5 %all-reduce.13 = (f32[]{:T(128)}, f32[]{:T(128)}) all-reduce(f32[]{:T(128)} %get-tuple-element.225, f32[]{:T(128)} %get-tuple-element.226), channel_id=1, replica_groups=mesh['region_0'=4,'region_1'=4,'region_2'=2,'blk'=4] {'region_1'}, use_global_device_ids=true, to_apply=%region_16.0 | all-reduce | flops 2 | bytes 16 | tf_op jit(solution)/shard_map/while/body/eval_jaxpr/psum | solution.py:53
  231.6 7.5 all-reduce.15
  245.9 5.7 fusion.51
  255.5 4.4 all-to-all-done
  272.9 7.2 all-reduce.12
  280.2 16.5 %all-reduce.13 = (f32[]{:T(128)}, f32[]{:T(128)}) all-reduce(f32[]{:T(128)} %get-tuple-element.225, f32[]{:T(128)} %get-tuple-element.226), channel_id=1, replica_groups=mesh['region_0'=4,'region_1'=4,'region_2'=2,'blk'=4] {'region_1'}, use_global_device_ids=true, to_apply=%region_16.0 | all-reduce | flops 2 | bytes 16 | tf_op jit(solution)/shard_map/while/body/eval_jaxpr/psum | solution.py:53
  299.9 7.5 all-reduce.15
  314.1 5.7 fusion.51
  323.7 4.4 all-to-all-done
  341.2 7.2 all-reduce.12
  348.4 16.5 %all-reduce.13 = (f32[]{:T(128)}, f32[]{:T(128)}) all-reduce(f32[]{:T(128)} %get-tuple-element.225, f32[]{:T(128)} %get-tuple-element.226), channel_id=1, replica_groups=mesh['region_0'=4,'region_1'=4,'region_2'=2,'blk'=4] {'region_1'}, use_global_device_ids=true, to_apply=%region_16.0 | all-reduce | flops 2 | bytes 16 | tf_op jit(solution)/shard_map/while/body/eval_jaxpr/psum | solution.py:53
  368.1 7.5 all-reduce.15
  382.3 5.7 fusion.51
  392.0 4.4 all-to-all-done
  409.4 7.2 all-reduce.12
  416.7 16.5 %all-reduce.13 = (f32[]{:T(128)}, f32[]{:T(128)}) all-reduce(f32[]{:T(128)} %get-tuple-element.225, f32[]{:T(128)} %get-tuple-element.226), channel_id=1, replica_groups=mesh['region_0'=4,'region_1'=4,'region_2'=2,'blk'=4] {'region_1'}, use_global_device_ids=true, to_apply=%region_16.0 | all-reduce | flops 2 | bytes 16 | tf_op jit(solution)/shard_map/while/body/eval_jaxpr/psum | solution.py:53
  436.3 7.5 all-reduce.15
  450.6 5.7 fusion.51
  460.2 4.4 all-to-all-done
  477.7 7.2 all-reduce.12
  484.9 16.5 %all-reduce.13 = (f32[]{:T(128)}, f32[]{:T(128)}) all-reduce(f32[]{:T(128)} %get-tuple-element.225, f32[]{:T(128)} %get-tuple-element.226), channel_id=1, replica_groups=mesh['region_0'=4,'region_1'=4,'region_2'=2,'blk'=4] {'region_1'}, use_global_device_ids=true, to_apply=%region_16.0 | all-reduce | flops 2 | bytes 16 | tf_op jit(solution)/shard_map/while/body/eval_jaxpr/psum | solution.py:53
  504.6 7.5 all-reduce.15
  518.8 5.7 fusion.51
  528.5 4.4 all-to-all-done
  545.9 7.2 all-reduce.12
  553.2 16.5 %all-reduce.13 = (f32[]{:T(128)}, f32[]{:T(128)}) all-reduce(f32[]{:T(128)} %get-tuple-element.225, f32[]{:T(128)} %get-tuple-element.226), channel_id=1, replica_groups=mesh['region_0'=4,'region_1'=4,'region_2'=2,'blk'=4] {'region_1'}, use_global_device_ids=true, to_apply=%region_16.0 | all-reduce | flops 2 | bytes 16 | tf_op jit(solution)/shard_map/while/body/eval_jaxpr/psum | solution.py:53
  572.8 7.5 all-reduce.15
  587.1 5.7 fusion.51
  614.2 7.2 all-reduce.12
  621.4 16.5 %all-reduce.13 = (f32[]{:T(128)}, f32[]{:T(128)}) all-reduce(f32[]{:T(128)} %get-tuple-element.225, f32[]{:T(128)} %get-tuple-element.226), channel_id=1, replica_groups=mesh['region_0'=4,'region_1'=4,'region_2'=2,'blk'=4] {'region_1'}, use_global_device_ids=true, to_apply=%region_16.0 | all-reduce | flops 2 | bytes 16 | tf_op jit(solution)/shard_map/while/body/eval_jaxpr/psum | solution.py:53
  641.1 7.5 all-reduce.15
  655.3 5.7 fusion.51
  682.4 7.2 all-reduce.12
  689.7 16.5 %all-reduce.13 = (f32[]{:T(128)}, f32[]{:T(128)}) all-reduce(f32[]{:T(128)} %get-tuple-element.225, f32[]{:T(128)} %get-tuple-element.226), channel_id=1, replica_groups=mesh['region_0'=4,'region_1'=4,'region_2'=2,'blk'=4] {'region_1'}, use_global_device_ids=true, to_apply=%region_16.0 | all-reduce | flops 2 | bytes 16 | tf_op jit(solution)/shard_map/while/body/eval_jaxpr/psum | solution.py:53
  709.3 7.5 all-reduce.15
  723.6 5.7 fusion.51
  733.2 4.4 all-to-all-done
  750.7 7.2 all-reduce.12
  757.9 16.5 %all-reduce.13 = (f32[]{:T(128)}, f32[]{:T(128)}) all-reduce(f32[]{:T(128)} %get-tuple-element.225, f32[]{:T(128)} %get-tuple-element.226), channel_id=1, replica_groups=mesh['region_0'=4,'region_1'=4,'region_2'=2,'blk'=4] {'region_1'}, use_global_device_ids=true, to_apply=%region_16.0 | all-reduce | flops 2 | bytes 16 | tf_op jit(solution)/shard_map/while/body/eval_jaxpr/psum | solution.py:53
  777.6 7.5 all-reduce.15
  791.8 5.7 fusion.51
  801.4 4.4 all-to-all-done
  818.9 7.2 all-reduce.12
  826.1 16.5 %all-reduce.13 = (f32[]{:T(128)}, f32[]{:T(128)}) all-reduce(f32[]{:T(128)} %get-tuple-element.225, f32[]{:T(128)} %get-tuple-element.226), channel_id=1, replica_groups=mesh['region_0'=4,'region_1'=4,'region_2'=2,'blk'=4] {'region_1'}, use_global_device_ids=true, to_apply=%region_16.0 | all-reduce | flops 2 | bytes 16 | tf_op jit(solution)/shard_map/while/body/eval_jaxpr/psum | solution.py:53
  845.8 7.5 all-reduce.15
  (356 shorter events, 305.7 us)
Async XLA Ops:
  0.6 32.2 %copy-start.1 = (f32[8,128]{1,0:T(8,128)S(1)}, f32[8,128]{1,0:T(8,128)}, u32[]{:S(2)}) copy-start(f32[8,128]{1,0:T(8,128)} %param.10) | copy-start | bytes 12292
  2.0 9.0 %all-to-all-start.1 = ((s32[4,8,8]{1,2,0:T(8,128)}), s32[4,8,8]{1,2,0:T(8,128)S(1)}, u32[]{:S(2)}, u32[]{:S(2)}) async-start(s32[4,8,8]{1,2,0:T(8,128)} %broadcast_in_dim.25), calls=%async_computation.1 | async-start | bytes 32768 | tf_op jit(solution)/shard_map/all_to_all | solution.py:34
  12.6 7.4 all-to-all-start.2
  25.4 5.8 collective-permute-start.4
  28.8 4.0 collective-permute-start.5
  32.8 6.4 collective-permute-start.6
  33.2 6.3 collective-permute-start.7
  57.7 7.5 collective-permute-start.8
  64.4 4.5 collective-permute-start.9
  103.9 5.3 collective-permute-start
  106.3 2.9 collective-permute-start.1
  116.2 7.7 all-to-all-start
  129.0 6.6 collective-permute-start.2
  132.0 3.7 collective-permute-start.3
  173.4 3.6 collective-permute-start
  175.7 1.3 collective-permute-start.1
  183.9 7.7 all-to-all-start
  196.8 7.0 collective-permute-start.2
  199.8 4.2 collective-permute-start.3
  241.7 3.6 collective-permute-start
  243.9 1.3 collective-permute-start.1
  252.2 7.7 all-to-all-start
  265.0 7.0 collective-permute-start.2
  268.1 4.2 collective-permute-start.3
  309.9 3.6 collective-permute-start
  312.2 1.3 collective-permute-start.1
  320.4 7.7 all-to-all-start
  333.3 7.0 collective-permute-start.2
  336.3 4.2 collective-permute-start.3
  378.2 3.6 collective-permute-start
  380.4 1.3 collective-permute-start.1
  388.7 7.7 all-to-all-start
  401.5 7.0 collective-permute-start.2
  404.6 4.2 collective-permute-start.3
  446.4 3.6 collective-permute-start
  448.7 1.3 collective-permute-start.1
  456.9 7.7 all-to-all-start
  469.8 7.0 collective-permute-start.2
  472.8 4.2 collective-permute-start.3
  514.7 3.6 collective-permute-start
  516.9 1.3 collective-permute-start.1
  525.2 7.7 all-to-all-start
  538.0 7.0 collective-permute-start.2
  541.0 4.2 collective-permute-start.3
  582.9 3.6 collective-permute-start
  585.2 1.3 collective-permute-start.1
  593.4 7.7 all-to-all-start
  606.3 7.0 collective-permute-start.2
  609.3 4.2 collective-permute-start.3
  651.1 3.6 collective-permute-start
  653.4 1.3 collective-permute-start.1
  661.6 7.7 all-to-all-start
  674.5 7.0 collective-permute-start.2
  677.5 4.2 collective-permute-start.3
  719.4 3.6 collective-permute-start
  721.6 1.3 collective-permute-start.1
  729.9 7.7 all-to-all-start
  742.7 7.0 collective-permute-start.2
  745.8 4.2 collective-permute-start.3
  787.6 3.6 collective-permute-start
  789.9 1.3 collective-permute-start.1
  798.1 7.7 all-to-all-start
  811.0 7.0 collective-permute-start.2
  814.0 4.2 collective-permute-start.3
  (3 other events, 33.3 us)
where the time goes:
time: 861 us; the launch traced here: 856 us
  blocking collectives  418 us (49%)
  starting transfers between devices  159 us (18%)
  matrix products  124 us (14%)
  waiting for transfers between devices  76.1 us (9%)
  loops' own time  35.5 us (4%)
  local copies, waits for them, and re-layouts  22.2 us (3%)
  other arithmetic  18.8 us (2%)
    psum x48, blocking collectives, over_axes(): return functools.reduce(lax.psum, axes, array)  412 us
    ppermute x26, starting transfers between devices, from_behind(): lax.ppermute(array, axis, [(i, (i + by) % length) for i in range(length)])  81.4 us
    dot_general x12, matrix products, branch_rows(): jnp.einsum('tjab,tjb->ta', jac_bus, flat[index], precision=hp)  68.1 us
    all_to_all x13, waiting for transfers between devices, sent_to_all(): return lax.all_to_all(copies, axis, split_axis=0, concat_axis=0, tiled=True)  57.1 us
    dot_general x13, matrix products, spread(): jnp.einsum('tjab,ta->tjb', tiles, weight, precision=lax.Precision.HIGHEST)  56 us
    all_to_all x13, starting transfers between devices, sent_to_all(): return lax.all_to_all(copies, axis, split_axis=0, concat_axis=0, tiled=True)  44.2 us
    another operation x1, loops' own time, body(): lax.fori_loop(0, ITERS - 1, one_step, (solution, residual, direction, alo...  35.5 us
    ppermute x12, starting transfers between devices, extended(): after = lax.ppermute(leading, axis, down)  30.5 us
  transfers between devices with their start and end apart: 63, of which 41 were waited for; matrix products, arithmetic and copies ran while one was open for 1% of the time, Pallas kernels for 0%

commit v1 on v0

v1 whole, which is shorter than its diff:
```python
import jax
import jax.numpy as jnp
from jax import lax
from jax.experimental import pallas as pl
from jax.experimental.pallas import tpu as pltpu
from jax.sharding import PartitionSpec as P

ITERS = 12
MESH = pl.DeviceIdType.MESH


def kernel(
    n_reg, n_blk,
    jac_hbm, pattern_ref, weight_ref, diag_ref, rhs_ref,
    sol_ref, res_ref,
    jac, pv, psm, wv, hsend, hbuf, oht, stage, back, uv, diag, xbuf, csend, rlo16, rhi16, rlo8, rhi8, dbuf,
    jsem, psem, gsend, grecv, hsend_sem, hrecv, xsend, xrecv, rsend, rrecv, dsend, drecv,
):
    reg = lax.axis_index("region")
    blk = lax.axis_index("blk")

    def region_at(k):
        return lax.rem(reg + k + n_reg, n_reg)

    def blk_at(k):
        return lax.rem(blk + k, n_blk)

    def to_blk(k):
        return (reg, blk_at(k))

    def to_reg(k):
        return (region_at(k), blk)

    def remote(src, dst, ssem, rsem, dev):
        return pltpu.make_async_remote_copy(
            src_ref=src, dst_ref=dst, send_sem=ssem, recv_sem=rsem,
            device_id=dev, device_id_type=MESH,
        )

    jcopies = [
        pltpu.make_async_copy(jac_hbm.at[pl.ds(8 * g, 8)], jac.at[pl.ds(8 * g, 8)], jsem.at[g])
        for g in range(4)
    ]
    for c in jcopies:
        c.start()

    barrier = pltpu.get_barrier_semaphore()
    for k in range(1, n_reg):
        pl.semaphore_signal(barrier, inc=1, device_id=to_reg(k), device_id_type=MESH)
    for k in range(1, n_blk):
        pl.semaphore_signal(barrier, inc=1, device_id=to_blk(k), device_id_type=MESH)

    pv[blk] = jnp.zeros((8, 128), jnp.int32)
    pv[blk, :, 0:8] = pattern_ref[...]
    wv[blk] = weight_ref[...]
    hsend[0:8] = diag_ref[...]
    hsend[8:16] = rhs_ref[...]
    stage[...] = jnp.zeros((128, 128), jnp.float32)
    back[...] = jnp.zeros((128, 128), jnp.float32)
    pl.semaphore_wait(barrier, n_reg - 1 + n_blk - 1)

    gcopies = []
    for k in range(1, n_blk):
        gcopies.append(remote(pv.at[blk], pv.at[blk], gsend.at[0, k], grecv.at[0, k], to_blk(k)))
        gcopies.append(remote(wv.at[blk], wv.at[blk], gsend.at[1, k], grecv.at[1, k], to_blk(k)))
    hcopies = [
        remote(hsend, hbuf.at[0], hsend_sem.at[0], hrecv.at[0], to_reg(1)),
        remote(hsend, hbuf.at[1], hsend_sem.at[1], hrecv.at[1], to_reg(-1)),
    ]
    for c in gcopies + hcopies:
        c.start()
    for c in gcopies:
        c.wait_recv()
    pcopy = pltpu.make_async_copy(pv, psm, psem)
    pcopy.start()

    lane = lax.broadcasted_iota(jnp.int32, (1, 128), 1)
    patf = pv[...].astype(jnp.float32).reshape(32, 128)
    lanes32 = lax.broadcasted_iota(jnp.int32, (32, 128), 1)
    for j in range(2):
        col = jnp.sum(jnp.where(lanes32 == 2 * blk + j, patf, 0.0), axis=1, keepdims=True)
        stage[32 * j : 32 * j + 32] = jnp.where(lanes32.astype(jnp.float32) == col, 1.0, 0.0)
    oht[...] = stage[...].T[0:32].astype(jnp.bfloat16)
    weight = wv[...].reshape(32, 128)

    def transposed_pad(rows):
        stage[0:32] = rows
        stage[32:64] = jnp.zeros((32, 128), jnp.float32)
        return stage[...].T

    def backward(rows, square, par):
        cols = transposed_pad(rows)
        for t in range(32):
            wc = jnp.broadcast_to(cols[:, t : t + 1], (128, 128))
            for j in range(2):
                tile = jac[t, j]
                term = tile * wc
                if square:
                    term = term * tile
                back[32 * j + t : 32 * j + t + 1] = jnp.sum(term, axis=0, keepdims=True)
        whole = back[...]
        high = whole.astype(jnp.bfloat16)
        rest = whole - high.astype(jnp.float32)
        mid = rest.astype(jnp.bfloat16)
        low = (rest - mid.astype(jnp.float32)).astype(jnp.bfloat16)
        hot = oht[...]

        def pick(piece):
            return jnp.dot(hot, piece, preferred_element_type=jnp.float32)

        total = pick(high) + (pick(mid) + pick(low))
        csend[par] = total[0:24]

    def r_copies(par):
        return [
            remote(csend.at[par, pl.ds(16, 8)], rlo8.at[par], rsend.at[par, 0], rrecv.at[par, 0], to_reg(2)),
            remote(csend.at[par, pl.ds(0, 8)], rhi8.at[par], rsend.at[par, 1], rrecv.at[par, 1], to_reg(-2)),
            remote(csend.at[par, pl.ds(8, 16)], rlo16.at[par], rsend.at[par, 2], rrecv.at[par, 2], to_reg(1)),
            remote(csend.at[par, pl.ds(0, 16)], rhi16.at[par], rsend.at[par, 3], rrecv.at[par, 3], to_reg(-1)),
        ]

    def r_sum(par):
        before = rlo8[par] + rlo16[par, 0:8] + csend[par, 0:8]
        own = rlo16[par, 8:16] + csend[par, 8:16] + rhi16[par, 0:8]
        after = csend[par, 16:24] + rhi16[par, 8:16] + rhi8[par]
        return jnp.concatenate([before, own, after], axis=0)

    for c in jcopies:
        c.wait()
    backward(weight, True, 0)
    copies = r_copies(0)
    for c in copies:
        c.start()
    pcopy.wait()
    for c in hcopies:
        c.wait_recv()
    for c in copies:
        c.wait_recv()
    diag[...] = jnp.concatenate([hbuf[0, 0:8], hsend[0:8], hbuf[1, 0:8]], axis=0)
    resid0 = jnp.concatenate([hbuf[0, 8:16], hsend[8:16], hbuf[1, 8:16]], axis=0)
    inv = 1.0 / (diag[...] + r_sum(0))
    for c in copies + gcopies + hcopies:
        c.wait_send()

    zeros8 = jnp.zeros((8, 128), jnp.float32)
    zeros24 = jnp.zeros((24, 128), jnp.float32)
    one = jnp.ones((1, 1), jnp.float32)

    def fold(first, second):
        both = jnp.where(lane < 64, first, second)
        rest = jnp.where(lane < 64, second, first)
        return both + pltpu.roll(rest, 64, 1)

    def step(i, carry):
        solution, direction, resid, along, gamma_old, alpha_old = carry
        par = lax.rem(i, 2)
        rpar = lax.rem(i + 1, 2)
        scaled = inv * resid
        uv[...] = scaled
        own_u = scaled[8:16]
        first = jnp.sum(own_u * resid[8:16], axis=0, keepdims=True)
        second = jnp.sum(own_u * own_u * diag[8:16], axis=0, keepdims=True)
        xbuf[par, blk, 32:33] = fold(first, second)

        lanes = lax.broadcasted_iota(jnp.int32, (128, 128), 1)
        acc = jnp.zeros((128, 128), jnp.float32)
        for t in range(32):
            x0 = uv[pl.ds(psm[t // 8, t % 8, 2 * blk], 1), :]
            x1 = uv[pl.ds(psm[t // 8, t % 8, 2 * blk + 1], 1), :]
            both = jac[t, 0] * x0 + jac[t, 1] * x1
            acc = jnp.where(lanes == t, jnp.sum(both, axis=1, keepdims=True), acc)
        xbuf[par, blk, 0:32] = acc.T[0:32]
        xcopies = [
            remote(xbuf.at[par, blk], xbuf.at[par, blk], xsend.at[par, k], xrecv.at[par, k], to_blk(k))
            for k in (2, 1, 3)
        ]
        for c in xcopies:
            c.start()
        for c in xcopies:
            c.wait_recv()
        rows = xbuf[par, 0, 0:32] + xbuf[par, 1, 0:32] + xbuf[par, 2, 0:32] + xbuf[par, 3, 0:32]
        scal = xbuf[par, 0, 32:33] + xbuf[par, 1, 32:33] + xbuf[par, 2, 32:33] + xbuf[par, 3, 32:33]
        weighted = weight * rows
        energy = jnp.sum(weighted * rows, axis=0, keepdims=True)
        dbuf[par, reg] = scal + fold(jnp.zeros((1, 128), jnp.float32), energy)
        dcopies = [
            remote(dbuf.at[par, reg], dbuf.at[par, reg], dsend.at[par], drecv.at[par], to_reg(k))
            for k in range(1, n_reg)
        ]
        for c in dcopies:
            c.start()
        backward(weighted, False, rpar)
        rcopies = r_copies(rpar)
        for c in rcopies:
            c.start()
        for c in rcopies:
            c.wait_recv()
        image = diag[...] * scaled + r_sum(rpar)
        others = dbuf.at[par, pl.ds(0, n_reg - 1)]
        dall = remote(others, others, dsend.at[par], drecv.at[par], to_reg(1))
        dall.wait_recv()
        sums = jnp.sum(dbuf[par].reshape(n_reg, 128), axis=0, keepdims=True)
        gamma = jnp.sum(jnp.where(lane < 64, sums, 0.0), axis=1, keepdims=True)
        delta = jnp.sum(jnp.where(lane < 64, 0.0, sums), axis=1, keepdims=True)
        begun = jnp.where(i == 0, 0.0, 1.0)
        beta = begun * gamma / gamma_old
        alpha = gamma / (delta - beta * gamma / alpha_old)
        direction = own_u + beta * direction
        along = image + beta * along
        solution = solution + alpha * direction
        resid = resid - alpha * along
        for c in xcopies + rcopies + [dall]:
            c.wait_send()
        return (solution, direction, resid, along, gamma, alpha)

    carry = lax.fori_loop(0, ITERS, step, (zeros8, zeros8, resid0, zeros24, one, one))
    sol_ref[...] = carry[0]
    res_ref[...] = carry[2][8:16]


def solution(mesh):
    n_reg, n_blk = mesh.shape["region"], mesh.shape["blk"]
    f32 = jnp.float32

    def body(jac_bus, pattern, branch_weight, bus_diag, right_side):
        vmem = pl.BlockSpec(memory_space=pltpu.VMEM)
        shape = jax.ShapeDtypeStruct((8, 128), f32)
        dma = pltpu.SemaphoreType.DMA

        def call(*args):
            return kernel(n_reg, n_blk, *args)

        return pl.pallas_call(
            call,
            out_shape=(shape, shape),
            in_specs=[pl.BlockSpec(memory_space=pl.ANY)] + [vmem] * 4,
            out_specs=(vmem, vmem),
            scratch_shapes=[
                pltpu.VMEM((32, 2, 128, 128), f32),
                pltpu.VMEM((4, 8, 128), jnp.int32),
                pltpu.SMEM((4, 8, 128), jnp.int32),
                pltpu.VMEM((4, 8, 128), f32),
                pltpu.VMEM((16, 128), f32),
                pltpu.VMEM((2, 16, 128), f32),
                pltpu.VMEM((32, 128), jnp.bfloat16),
                pltpu.VMEM((128, 128), f32),
                pltpu.VMEM((128, 128), f32),
                pltpu.VMEM((24, 128), f32),
                pltpu.VMEM((24, 128), f32),
                pltpu.VMEM((2, 4, 40, 128), f32),
                pltpu.VMEM((2, 24, 128), f32),
                pltpu.VMEM((2, 16, 128), f32),
                pltpu.VMEM((2, 16, 128), f32),
                pltpu.VMEM((2, 8, 128), f32),
                pltpu.VMEM((2, 8, 128), f32),
                pltpu.VMEM((2, 32, 1, 128), f32),
                dma((4,)), dma, dma((2, 4)), dma((2, 4)), dma((2,)), dma((2,)),
                dma((2, 4)), dma((2, 4)), dma((2, 4)), dma((2, 4)), dma((2,)), dma((2,)),
            ],
            compiler_params=pltpu.CompilerParams(collective_id=0, has_side_effects=True),
            name="pcg",
        )(jac_bus, pattern, branch_weight, bus_diag, right_side)

    axes = ("region", "blk")
    in_specs = (P("region", "blk", None, None),) + (P(axes, None),) * 4
    return jax.shard_map(
        body, mesh=mesh, in_specs=in_specs, out_specs=(P(axes, None),) * 2, check_vma=False
    )
```

time: 861 us -> 142 us (0.16)
  blocking collectives: 418 us -> 0 us
  starting transfers between devices: 159 us -> 0 us
  Pallas kernels: 0 us -> 138 us
  matrix products: 124 us -> 0 us
  waiting for transfers between devices: 76.1 us -> 0 us
  loops' own time: 35.5 us -> 0 us
  local copies, waits for them, and re-layouts: 22.2 us -> 2.53 us
  other arithmetic: 18.8 us -> 0 us
    psum x48 -> x0, blocking collectives: 412 us -> none  [over_axes(): return functools.reduce(lax.psum, axes, array)]
    pallas_call x0 -> x1, Pallas kernels: none -> 138 us  [body(): pl.pallas_call(call, out_shape=(shape, shape), in_specs=[pl.BlockSpec(mem...]
    dot_general x25 -> x0, matrix products: 124 us -> none  [the longest x12 68.1 us: branch_rows(): jnp.einsum('tjab,tjb->ta', jac_bus, flat[index], precision=hp)]
    ppermute x50 -> x0, starting transfers between devices: 115 us -> none  [the longest x26 81.4 us: from_behind(): lax.ppermute(array, axis, [(i, (i + by) % length) for i in range(length)])]
    all_to_all x13 -> x0, waiting for transfers between devices: 57.1 us -> none  [sent_to_all(): return lax.all_to_all(copies, axis, split_axis=0, concat_axis=0, tiled=True)]
    all_to_all x13 -> x0, starting transfers between devices: 44.2 us -> none  [sent_to_all(): return lax.all_to_all(copies, axis, split_axis=0, concat_axis=0, tiled=True)]
    another operation x1 -> x0, loops' own time: 35.5 us -> none  [body(): lax.fori_loop(0, ITERS - 1, one_step, (solution, residual, direction, alo...]
    ppermute x50 -> x0, waiting for transfers between devices: 19 us -> none  [the longest x26 9.31 us: from_behind(): lax.ppermute(array, axis, [(i, (i + by) % length) for i in range(length)])]
  transfers between devices with their start and end apart: 63 -> 0, of which waited for: 41 -> 0; matrix products, arithmetic and copies ran while one was open for 1% -> 0% of each run, Pallas kernels for 0% -> 0%
where the time goes in v1:
time: 142 us; the launch traced here: 141 us
  Pallas kernels  138 us (97%)
  local copies, waits for them, and re-layouts  2.53 us (2%)
    pallas_call x1, Pallas kernels, body(): pl.pallas_call(call, out_shape=(shape, shape), in_specs=[pl.BlockSpec(mem...  138 us

profile of v1, /device:TPU:1, one launch (start us, length us, event | category | flops | bytes accessed | tf_op | source)
XLA Modules:
  0.0 141.2 jit_solution(10960737418518190471)
XLA Ops:
  0.6 138.0 %pcg.1 = (f32[8,128]{1,0:T(8,128)}, f32[8,128]{1,0:T(8,128)}) custom-call(f32[32,2,128,128]{3,2,1,0:T(8,128)} %args_0_.4, s32[8,8]{1,0:T(8,128)} %args_1_.4, f32[8,128]{1,0:T(8,128)} %args_2_.4, f32[8,128]{1,0:T(8,128)} %args_3_.4, f32[8,128]{1,0:T(8,128)} %args_4_.4), custom_call_target="tpu_custom_call" | custom-call | tf_op jit(solution)/shard_map/pcg/pallas_call | solution.py:233
  138.7 1.3 copy.9
  139.9 1.3 copy.10

commit v2 on v1

--- a/solution.py
+++ b/solution.py
@@ -9,11 +9,16 @@
 MESH = pl.DeviceIdType.MESH
 
 
+def farness(k):
+    along_z, along_y = min(k // 8, 4 - k // 8), min(k // 2 % 4, 4 - k // 2 % 4)
+    return along_z + along_y
+
+
 def kernel(
     n_reg, n_blk,
     jac_hbm, pattern_ref, weight_ref, diag_ref, rhs_ref,
     sol_ref, res_ref,
-    jac, pv, psm, wv, hsend, hbuf, oht, stage, back, uv, diag, xbuf, csend, rlo16, rhi16, rlo8, rhi8, dbuf,
+    jac, jhl, jsq, pv, psm, wv, hsend, hbuf, oht, stage, picked, uv, diag, xbuf, csend, rlo16, rhi16, rlo8, rhi8, dbuf,
     jsem, psem, gsend, grecv, hsend_sem, hrecv, xsend, xrecv, rsend, rrecv, dsend, drecv,
 ):
     reg = lax.axis_index("region")
@@ -55,8 +60,6 @@
     wv[blk] = weight_ref[...]
     hsend[0:8] = diag_ref[...]
     hsend[8:16] = rhs_ref[...]
-    stage[...] = jnp.zeros((128, 128), jnp.float32)
-    back[...] = jnp.zeros((128, 128), jnp.float32)
     pl.semaphore_wait(barrier, n_reg - 1 + n_blk - 1)
 
     gcopies = []
@@ -69,6 +72,25 @@
     ]
     for c in gcopies + hcopies:
         c.start()
+    def halves(value):
+        high = value.astype(jnp.bfloat16)
+        return high, (value - high.astype(jnp.float32)).astype(jnp.bfloat16)
+
+    def convert(t, _):
+        for j in range(2):
+            tile = jac[t, j]
+            high, low = halves(tile)
+            jhl[t, 0:128, 128 * j : 128 * j + 128] = high
+            jhl[t, 128:256, 128 * j : 128 * j + 128] = low
+            high, low = halves(tile * tile)
+            jsq[t, 0:128, 128 * j : 128 * j + 128] = high
+            jsq[t, 128:256, 128 * j : 128 * j + 128] = low
+        return 0
+
+    for c in jcopies:
+        c.wait()
+    lax.fori_loop(0, 32, convert, 0)
+
     for c in gcopies:
         c.wait_recv()
     pcopy = pltpu.make_async_copy(pv, psm, psem)
@@ -79,36 +101,39 @@
     lanes32 = lax.broadcasted_iota(jnp.int32, (32, 128), 1)
     for j in range(2):
         col = jnp.sum(jnp.where(lanes32 == 2 * blk + j, patf, 0.0), axis=1, keepdims=True)
-        stage[32 * j : 32 * j + 32] = jnp.where(lanes32.astype(jnp.float32) == col, 1.0, 0.0)
-    oht[...] = stage[...].T[0:32].astype(jnp.bfloat16)
+        hit = jnp.where(lanes32.astype(jnp.float32) == col, 1.0, 0.0)
+        stage[32 * j : 32 * j + 32] = hit
+        stage[64 + 32 * j : 96 + 32 * j] = hit
+    hot = stage[...].T[0:32]
+    oht[:, 0:128] = hot.astype(jnp.bfloat16)
+    oht[:, 128:256] = jnp.where(lanes32 < 64, hot, 0.0).astype(jnp.bfloat16)
     weight = wv[...].reshape(32, 128)
 
-    def transposed_pad(rows):
-        stage[0:32] = rows
-        stage[32:64] = jnp.zeros((32, 128), jnp.float32)
-        return stage[...].T
-
-    def backward(rows, square, par):
-        cols = transposed_pad(rows)
-        for t in range(32):
-            wc = jnp.broadcast_to(cols[:, t : t + 1], (128, 128))
-            for j in range(2):
-                tile = jac[t, j]
-                term = tile * wc
-                if square:
-                    term = term * tile
-                back[32 * j + t : 32 * j + t + 1] = jnp.sum(term, axis=0, keepdims=True)
-        whole = back[...]
+    rows16 = lax.rem(lax.broadcasted_iota(jnp.int32, (16, 256), 0), 8)
+
+    def group_products(lhs, mats, g, contract):
+        acc = jnp.zeros((16, 256), jnp.float32)
+        for k in range(8):
+            out = lax.dot_general(
+                lhs, mats[8 * g + k], (((1,), (contract,)), ((), ())),
+                preferred_element_type=jnp.float32,
+            )
+            acc = jnp.where(rows16 == k, out, acc)
+        return acc[8:16] + acc[0:8]
+
+    def backward(rows, mats, par):
+        parts = []
+        for g in range(4):
+            high, low = halves(rows[8 * g : 8 * g + 8])
+            both = jnp.concatenate([high.astype(jnp.float32), low.astype(jnp.float32)], axis=0)
+            lhs = jnp.concatenate([both, both], axis=1).astype(jnp.bfloat16)
+            parts.append(group_products(lhs, mats, g, 0))
+        whole = jnp.concatenate([p[:, 0:128] for p in parts] + [p[:, 128:256] for p in parts], axis=0)
         high = whole.astype(jnp.bfloat16)
         rest = whole - high.astype(jnp.float32)
-        mid = rest.astype(jnp.bfloat16)
-        low = (rest - mid.astype(jnp.float32)).astype(jnp.bfloat16)
-        hot = oht[...]
-
-        def pick(piece):
-            return jnp.dot(hot, piece, preferred_element_type=jnp.float32)
-
-        total = pick(high) + (pick(mid) + pick(low))
+        mid, low = halves(rest)
+        stack = jnp.concatenate([high, mid, low, jnp.zeros((64, 128), jnp.bfloat16)], axis=0)
+        total = jnp.dot(oht[...], stack, preferred_element_type=jnp.float32)
         csend[par] = total[0:24]
 
     def r_copies(par):
@@ -125,9 +150,7 @@
         after = csend[par, 16:24] + rhi16[par, 8:16] + rhi8[par]
         return jnp.concatenate([before, own, after], axis=0)
 
-    for c in jcopies:
-        c.wait()
-    backward(weight, True, 0)
+    backward(weight, jsq, 0)
     copies = r_copies(0)
     for c in copies:
         c.start()
@@ -142,6 +165,7 @@
     for c in copies + gcopies + hcopies:
         c.wait_send()
 
+    order = sorted(range(1, n_reg), key=farness, reverse=True)
     zeros8 = jnp.zeros((8, 128), jnp.float32)
     zeros24 = jnp.zeros((24, 128), jnp.float32)
     one = jnp.ones((1, 1), jnp.float32)
@@ -162,16 +186,18 @@
         second = jnp.sum(own_u * own_u * diag[8:16], axis=0, keepdims=True)
         xbuf[par, blk, 32:33] = fold(first, second)
 
-        lanes = lax.broadcasted_iota(jnp.int32, (128, 128), 1)
-        acc = jnp.zeros((128, 128), jnp.float32)
         for t in range(32):
-            x0 = uv[pl.ds(psm[t // 8, t % 8, 2 * blk], 1), :]
-            x1 = uv[pl.ds(psm[t // 8, t % 8, 2 * blk + 1], 1), :]
-            both = jac[t, 0] * x0 + jac[t, 1] * x1
-            acc = jnp.where(lanes == t, jnp.sum(both, axis=1, keepdims=True), acc)
-        xbuf[par, blk, 0:32] = acc.T[0:32]
+            for j in range(2):
+                source = pl.ds(psm[t // 8, t % 8, 2 * blk + j], 1)
+                picked[t : t + 1, 128 * j : 128 * j + 128] = uv[source, :]
+        for g in range(4):
+            value = picked[8 * g : 8 * g + 8]
+            high = value.astype(jnp.bfloat16).astype(jnp.float32)
+            lhs = jnp.concatenate([high, value - high], axis=0).astype(jnp.bfloat16)
+            out = group_products(lhs, jhl, g, 1)
+            xbuf[par, blk, 8 * g : 8 * g + 8] = out[:, 0:128] + out[:, 128:256]
         xcopies = [
-            remote(xbuf.at[par, blk], xbuf.at[par, blk], xsend.at[par, k], xrecv.at[par, k], to_blk(k))
+            remote(xbuf.at[par, blk, pl.ds(0, 33)], xbuf.at[par, blk, pl.ds(0, 33)], xsend.at[par, k], xrecv.at[par, k], to_blk(k))
             for k in (2, 1, 3)
         ]
         for c in xcopies:
@@ -185,11 +211,11 @@
         dbuf[par, reg] = scal + fold(jnp.zeros((1, 128), jnp.float32), energy)
         dcopies = [
             remote(dbuf.at[par, reg], dbuf.at[par, reg], dsend.at[par], drecv.at[par], to_reg(k))
-            for k in range(1, n_reg)
+            for k in order
         ]
         for c in dcopies:
             c.start()
-        backward(weighted, False, rpar)
+        backward(weighted, jhl, rpar)
         rcopies = r_copies(rpar)
         for c in rcopies:
             c.start()
@@ -237,14 +263,16 @@
             out_specs=(vmem, vmem),
             scratch_shapes=[
                 pltpu.VMEM((32, 2, 128, 128), f32),
+                pltpu.VMEM((32, 256, 256), jnp.bfloat16),
+                pltpu.VMEM((32, 256, 256), jnp.bfloat16),
                 pltpu.VMEM((4, 8, 128), jnp.int32),
                 pltpu.SMEM((4, 8, 128), jnp.int32),
                 pltpu.VMEM((4, 8, 128), f32),
                 pltpu.VMEM((16, 128), f32),
                 pltpu.VMEM((2, 16, 128), f32),
-                pltpu.VMEM((32, 128), jnp.bfloat16),
+                pltpu.VMEM((32, 256), jnp.bfloat16),
                 pltpu.VMEM((128, 128), f32),
-                pltpu.VMEM((128, 128), f32),
+                pltpu.VMEM((32, 256), f32),
                 pltpu.VMEM((24, 128), f32),
                 pltpu.VMEM((24, 128), f32),
                 pltpu.VMEM((2, 4, 40, 128), f32),

time: 142 us -> 142 us (level)
  no operation moved by 1% of the time
where the time goes in v2:
time: 142 us
  Pallas kernels  139 us (98%)
  local copies, waits for them, and re-layouts  2.53 us (2%)
    pallas_call x1, Pallas kernels, body(): pl.pallas_call(call, out_shape=(shape, shape), in_specs=[pl.BlockSpec(mem...  139 us

profile of v2, /device:TPU:1, one launch (start us, length us, event | category | flops | bytes accessed | tf_op | source)
XLA Modules:
  0.0 141.9 jit_solution(16025626716186005805)
XLA Ops:
  0.6 138.8 %pcg.1 = (f32[8,128]{1,0:T(8,128)}, f32[8,128]{1,0:T(8,128)}) custom-call(f32[32,2,128,128]{3,2,1,0:T(8,128)} %args_0_.4, s32[8,8]{1,0:T(8,128)} %args_1_.4, f32[8,128]{1,0:T(8,128)} %args_2_.4, f32[8,128]{1,0:T(8,128)} %args_3_.4, f32[8,128]{1,0:T(8,128)} %args_4_.4), custom_call_target="tpu_custom_call" | custom-call | tf_op jit(solution)/shard_map/pcg/pallas_call | solution.py:259
  139.4 1.3 copy.9
  140.7 1.3 copy.10

commit v3 on v1

--- a/solution.py
+++ b/solution.py
@@ -9,11 +9,16 @@
 MESH = pl.DeviceIdType.MESH
 
 
+def farness(k):
+    along_z, along_y = min(k // 8, 4 - k // 8), min(k // 2 % 4, 4 - k // 2 % 4)
+    return along_z + along_y
+
+
 def kernel(
     n_reg, n_blk,
     jac_hbm, pattern_ref, weight_ref, diag_ref, rhs_ref,
     sol_ref, res_ref,
-    jac, pv, psm, wv, hsend, hbuf, oht, stage, back, uv, diag, xbuf, csend, rlo16, rhi16, rlo8, rhi8, dbuf,
+    jac, pv, psm, wv, hsend, hbuf, oht, stage, part, uv, diag, xbuf, csend, rlo16, rhi16, rlo8, rhi8, dbuf,
     jsem, psem, gsend, grecv, hsend_sem, hrecv, xsend, xrecv, rsend, rrecv, dsend, drecv,
 ):
     reg = lax.axis_index("region")
@@ -55,8 +60,6 @@
     wv[blk] = weight_ref[...]
     hsend[0:8] = diag_ref[...]
     hsend[8:16] = rhs_ref[...]
-    stage[...] = jnp.zeros((128, 128), jnp.float32)
-    back[...] = jnp.zeros((128, 128), jnp.float32)
     pl.semaphore_wait(barrier, n_reg - 1 + n_blk - 1)
 
     gcopies = []
@@ -79,36 +82,42 @@
     lanes32 = lax.broadcasted_iota(jnp.int32, (32, 128), 1)
     for j in range(2):
         col = jnp.sum(jnp.where(lanes32 == 2 * blk + j, patf, 0.0), axis=1, keepdims=True)
-        stage[32 * j : 32 * j + 32] = jnp.where(lanes32.astype(jnp.float32) == col, 1.0, 0.0)
-    oht[...] = stage[...].T[0:32].astype(jnp.bfloat16)
+        hit = jnp.where(lanes32.astype(jnp.float32) == col, 1.0, 0.0)
+        stage[32 * j : 32 * j + 32] = hit
+        stage[64 + 32 * j : 96 + 32 * j] = hit
+    hot = stage[...].T[0:32]
+    oht[:, 0:128] = hot.astype(jnp.bfloat16)
+    oht[:, 128:256] = jnp.where(lanes32 < 64, hot, 0.0).astype(jnp.bfloat16)
     weight = wv[...].reshape(32, 128)
 
-    def transposed_pad(rows):
-        stage[0:32] = rows
-        stage[32:64] = jnp.zeros((32, 128), jnp.float32)
-        return stage[...].T
+    def eight_sums(terms):
+        total = terms[0:8]
+        for k in range(1, 16):
+            total = total + terms[8 * k : 8 * k + 8]
+        return total
+
+    def group_rows(slot):
+        total = part[slot, pl.ds(0, 8, stride=8), :]
+        for k in range(1, 8):
+            total = total + part[slot, pl.ds(k, 8, stride=8), :]
+        return total
 
     def backward(rows, square, par):
-        cols = transposed_pad(rows)
         for t in range(32):
-            wc = jnp.broadcast_to(cols[:, t : t + 1], (128, 128))
+            wc = jnp.broadcast_to(rows[t : t + 1], (128, 128)).T
             for j in range(2):
                 tile = jac[t, j]
                 term = tile * wc
                 if square:
                     term = term * tile
-                back[32 * j + t : 32 * j + t + 1] = jnp.sum(term, axis=0, keepdims=True)
-        whole = back[...]
+                part[4 * j + t // 8, 8 * (t % 8) : 8 * (t % 8) + 8] = eight_sums(term)
+        whole = jnp.concatenate([group_rows(k) for k in range(8)], axis=0)
         high = whole.astype(jnp.bfloat16)
         rest = whole - high.astype(jnp.float32)
         mid = rest.astype(jnp.bfloat16)
         low = (rest - mid.astype(jnp.float32)).astype(jnp.bfloat16)
-        hot = oht[...]
-
-        def pick(piece):
-            return jnp.dot(hot, piece, preferred_element_type=jnp.float32)
-
-        total = pick(high) + (pick(mid) + pick(low))
+        stack = jnp.concatenate([high, mid, low, jnp.zeros((64, 128), jnp.bfloat16)], axis=0)
+        total = jnp.dot(oht[...], stack, preferred_element_type=jnp.float32)
         csend[par] = total[0:24]
 
     def r_copies(par):
@@ -142,6 +151,7 @@
     for c in copies + gcopies + hcopies:
         c.wait_send()
 
+    order = sorted(range(1, n_reg), key=farness, reverse=True)
     zeros8 = jnp.zeros((8, 128), jnp.float32)
     zeros24 = jnp.zeros((24, 128), jnp.float32)
     one = jnp.ones((1, 1), jnp.float32)
@@ -162,16 +172,15 @@
         second = jnp.sum(own_u * own_u * diag[8:16], axis=0, keepdims=True)
         xbuf[par, blk, 32:33] = fold(first, second)
 
-        lanes = lax.broadcasted_iota(jnp.int32, (128, 128), 1)
-        acc = jnp.zeros((128, 128), jnp.float32)
         for t in range(32):
             x0 = uv[pl.ds(psm[t // 8, t % 8, 2 * blk], 1), :]
             x1 = uv[pl.ds(psm[t // 8, t % 8, 2 * blk + 1], 1), :]
             both = jac[t, 0] * x0 + jac[t, 1] * x1
-            acc = jnp.where(lanes == t, jnp.sum(both, axis=1, keepdims=True), acc)
-        xbuf[par, blk, 0:32] = acc.T[0:32]
+            part[t // 8, 8 * (t % 8) : 8 * (t % 8) + 8] = eight_sums(both.T)
+        for g in range(4):
+            xbuf[par, blk, 8 * g : 8 * g + 8] = group_rows(g)
         xcopies = [
-            remote(xbuf.at[par, blk], xbuf.at[par, blk], xsend.at[par, k], xrecv.at[par, k], to_blk(k))
+            remote(xbuf.at[par, blk, pl.ds(0, 33)], xbuf.at[par, blk, pl.ds(0, 33)], xsend.at[par, k], xrecv.at[par, k], to_blk(k))
             for k in (2, 1, 3)
         ]
         for c in xcopies:
@@ -185,7 +194,7 @@
         dbuf[par, reg] = scal + fold(jnp.zeros((1, 128), jnp.float32), energy)
         dcopies = [
             remote(dbuf.at[par, reg], dbuf.at[par, reg], dsend.at[par], drecv.at[par], to_reg(k))
-            for k in range(1, n_reg)
+            for k in order
         ]
         for c in dcopies:
             c.start()
@@ -242,9 +251,9 @@
                 pltpu.VMEM((4, 8, 128), f32),
                 pltpu.VMEM((16, 128), f32),
                 pltpu.VMEM((2, 16, 128), f32),
-                pltpu.VMEM((32, 128), jnp.bfloat16),
+                pltpu.VMEM((32, 256), jnp.bfloat16),
                 pltpu.VMEM((128, 128), f32),
-                pltpu.VMEM((128, 128), f32),
+                pltpu.VMEM((8, 64, 128), f32),
                 pltpu.VMEM((24, 128), f32),
                 pltpu.VMEM((24, 128), f32),
                 pltpu.VMEM((2, 4, 40, 128), f32),

time: 142 us -> 133 us (0.937)
  Pallas kernels: 138 us -> 130 us
    pallas_call x1, Pallas kernels: 138 us -> 130 us  [body(): pl.pallas_call(call, out_shape=(shape, shape), in_specs=[pl.BlockSpec(mem...]
where the time goes in v3:
time: 133 us
  Pallas kernels  130 us (98%)
  local copies, waits for them, and re-layouts  2.53 us (2%)
    pallas_call x1, Pallas kernels, body(): pl.pallas_call(call, out_shape=(shape, shape), in_specs=[pl.BlockSpec(mem...  130 us

profile of v3, /device:TPU:1, one launch (start us, length us, event | category | flops | bytes accessed | tf_op | source)
XLA Modules:
  0.0 133.2 jit_solution(14292660269327584701)
XLA Ops:
  0.6 130.0 %pcg.1 = (f32[8,128]{1,0:T(8,128)}, f32[8,128]{1,0:T(8,128)}) custom-call(f32[32,2,128,128]{3,2,1,0:T(8,128)} %args_0_.4, s32[8,8]{1,0:T(8,128)} %args_1_.4, f32[8,128]{1,0:T(8,128)} %args_2_.4, f32[8,128]{1,0:T(8,128)} %args_3_.4, f32[8,128]{1,0:T(8,128)} %args_4_.4), custom_call_target="tpu_custom_call" | custom-call | tf_op jit(solution)/shard_map/pcg/pallas_call | solution.py:242
  130.7 1.3 copy.9
  132.0 1.3 copy.10

commit v4 on v3

--- a/solution.py
+++ b/solution.py
@@ -6,6 +6,8 @@
 from jax.sharding import PartitionSpec as P
 
 ITERS = 12
+CHUNKS = 2
+SPAN = 32 // CHUNKS
 MESH = pl.DeviceIdType.MESH
 
 
@@ -16,10 +18,10 @@
 
 def kernel(
     n_reg, n_blk,
-    jac_hbm, pattern_ref, weight_ref, diag_ref, rhs_ref,
-    sol_ref, res_ref,
-    jac, pv, psm, wv, hsend, hbuf, oht, stage, part, uv, diag, xbuf, csend, rlo16, rhi16, rlo8, rhi8, dbuf,
-    jsem, psem, gsend, grecv, hsend_sem, hrecv, xsend, xrecv, rsend, rrecv, dsend, drecv,
+    jac_hbm, pattern_hbm, weight_hbm, diag_hbm, rhs_hbm,
+    out_ref,
+    jac, pat, pv, psm, wv, hsend, hbuf, oht, stage, part, uv, diag, xbuf, csend, rlo16, rhi16, rlo8, rhi8, dbuf,
+    jsem, isem, far_sem, psem, gsend, grecv, hsend_sem, hrecv, xsend, xrecv, rsend, rrecv, dsend, drecv,
 ):
     reg = lax.axis_index("region")
     blk = lax.axis_index("blk")
@@ -46,21 +48,29 @@
         pltpu.make_async_copy(jac_hbm.at[pl.ds(8 * g, 8)], jac.at[pl.ds(8 * g, 8)], jsem.at[g])
         for g in range(4)
     ]
-    for c in jcopies:
+    icopies = [
+        pltpu.make_async_copy(pattern_hbm, pat, isem.at[0]),
+        pltpu.make_async_copy(weight_hbm, wv.at[blk], isem.at[1]),
+        pltpu.make_async_copy(diag_hbm, hsend.at[pl.ds(0, 8)], isem.at[2]),
+        pltpu.make_async_copy(rhs_hbm, hsend.at[pl.ds(8, 8)], isem.at[3]),
+    ]
+    for c in icopies + jcopies:
         c.start()
 
     barrier = pltpu.get_barrier_semaphore()
-    for k in range(1, n_reg):
-        pl.semaphore_signal(barrier, inc=1, device_id=to_reg(k), device_id_type=MESH)
-    for k in range(1, n_blk):
-        pl.semaphore_signal(barrier, inc=1, device_id=to_blk(k), device_id_type=MESH)
+    near = [to_blk(k) for k in range(1, n_blk)] + [to_reg(k) for k in (1, -1, 2, -2)]
+    for dev in near:
+        pl.semaphore_signal(barrier, inc=1, device_id=dev, device_id_type=MESH)
+
+    def far_signal(n):
+        for k in (2 << n, -(2 << n)):
+            pl.semaphore_signal(far_sem.at[n], inc=1, device_id=to_reg(k), device_id_type=MESH)
 
     pv[blk] = jnp.zeros((8, 128), jnp.int32)
-    pv[blk, :, 0:8] = pattern_ref[...]
-    wv[blk] = weight_ref[...]
-    hsend[0:8] = diag_ref[...]
-    hsend[8:16] = rhs_ref[...]
-    pl.semaphore_wait(barrier, n_reg - 1 + n_blk - 1)
+    for c in icopies:
+        c.wait()
+    pv[blk, :, 0:8] = pat[...]
+    pl.semaphore_wait(barrier, len(near))
 
     gcopies = []
     for k in range(1, n_blk):
@@ -72,6 +82,9 @@
     ]
     for c in gcopies + hcopies:
         c.start()
+    far_signal(0)
+    pl.semaphore_wait(far_sem.at[0], 2)
+    far_signal(1)
     for c in gcopies:
         c.wait_recv()
     pcopy = pltpu.make_async_copy(pv, psm, psem)
@@ -102,15 +115,17 @@
             total = total + part[slot, pl.ds(k, 8, stride=8), :]
         return total
 
-    def backward(rows, square, par):
-        for t in range(32):
-            wc = jnp.broadcast_to(rows[t : t + 1], (128, 128)).T
+    def backward_tiles(first, rows, square):
+        for t in range(first, first + rows.shape[0]):
+            wc = jnp.broadcast_to(rows[t - first : t - first + 1], (128, 128)).T
             for j in range(2):
                 tile = jac[t, j]
                 term = tile * wc
                 if square:
                     term = term * tile
                 part[4 * j + t // 8, 8 * (t % 8) : 8 * (t % 8) + 8] = eight_sums(term)
+
+    def backward_end(par):
         whole = jnp.concatenate([group_rows(k) for k in range(8)], axis=0)
         high = whole.astype(jnp.bfloat16)
         rest = whole - high.astype(jnp.float32)
@@ -136,10 +151,13 @@
 
     for c in jcopies:
         c.wait()
-    backward(weight, True, 0)
+    backward_tiles(0, weight, True)
+    backward_end(0)
     copies = r_copies(0)
     for c in copies:
         c.start()
+    pl.semaphore_wait(far_sem.at[1], 2)
+    far_signal(2)
     pcopy.wait()
     for c in hcopies:
         c.wait_recv()
@@ -150,6 +168,7 @@
     inv = 1.0 / (diag[...] + r_sum(0))
     for c in copies + gcopies + hcopies:
         c.wait_send()
+    pl.semaphore_wait(far_sem.at[2], 2)
 
     order = sorted(range(1, n_reg), key=farness, reverse=True)
     zeros8 = jnp.zeros((8, 128), jnp.float32)
@@ -170,35 +189,46 @@
         own_u = scaled[8:16]
         first = jnp.sum(own_u * resid[8:16], axis=0, keepdims=True)
         second = jnp.sum(own_u * own_u * diag[8:16], axis=0, keepdims=True)
-        xbuf[par, blk, 32:33] = fold(first, second)
-
-        for t in range(32):
-            x0 = uv[pl.ds(psm[t // 8, t % 8, 2 * blk], 1), :]
-            x1 = uv[pl.ds(psm[t // 8, t % 8, 2 * blk + 1], 1), :]
-            both = jac[t, 0] * x0 + jac[t, 1] * x1
-            part[t // 8, 8 * (t % 8) : 8 * (t % 8) + 8] = eight_sums(both.T)
-        for g in range(4):
-            xbuf[par, blk, 8 * g : 8 * g + 8] = group_rows(g)
-        xcopies = [
-            remote(xbuf.at[par, blk, pl.ds(0, 33)], xbuf.at[par, blk, pl.ds(0, 33)], xsend.at[par, k], xrecv.at[par, k], to_blk(k))
-            for k in (2, 1, 3)
-        ]
-        for c in xcopies:
-            c.start()
-        for c in xcopies:
-            c.wait_recv()
-        rows = xbuf[par, 0, 0:32] + xbuf[par, 1, 0:32] + xbuf[par, 2, 0:32] + xbuf[par, 3, 0:32]
-        scal = xbuf[par, 0, 32:33] + xbuf[par, 1, 32:33] + xbuf[par, 2, 32:33] + xbuf[par, 3, 32:33]
-        weighted = weight * rows
-        energy = jnp.sum(weighted * rows, axis=0, keepdims=True)
-        dbuf[par, reg] = scal + fold(jnp.zeros((1, 128), jnp.float32), energy)
+        xbuf[par, blk, SPAN : SPAN + 1] = fold(first, second)
+
+        xcopies = []
+        for c in range(CHUNKS):
+            for t in range(SPAN * c, SPAN * c + SPAN):
+                x0 = uv[pl.ds(psm[t // 8, t % 8, 2 * blk], 1), :]
+                x1 = uv[pl.ds(psm[t // 8, t % 8, 2 * blk + 1], 1), :]
+                both = jac[t, 0] * x0 + jac[t, 1] * x1
+                part[t // 8, 8 * (t % 8) : 8 * (t % 8) + 8] = eight_sums(both.T)
+            at = SPAN * c + (8 if c else 0)
+            for g in range(SPAN // 8):
+                xbuf[par, blk, at + 8 * g : at + 8 * g + 8] = group_rows(SPAN // 8 * c + g)
+            mine = xbuf.at[par, blk, pl.ds(at, SPAN if c else SPAN + 1)]
+            xcopies.append([
+                remote(mine, mine, xsend.at[par, c, k], xrecv.at[par, c, k], to_blk(k))
+                for k in (2, 1, 3)
+            ])
+            for copy in xcopies[c]:
+                copy.start()
+        energy = jnp.zeros((1, 128), jnp.float32)
+        for c in range(CHUNKS):
+            for copy in xcopies[c]:
+                copy.wait_recv()
+            at = SPAN * c + (8 if c else 0)
+            b0, b1, b2, b3 = (xbuf[par, b, at : at + SPAN] for b in range(4))
+            rows = b0 + b1 + b2 + b3
+            weighted = weight[SPAN * c : SPAN * c + SPAN] * rows
+            energy = energy + jnp.sum(weighted * rows, axis=0, keepdims=True)
+            if c < CHUNKS - 1:
+                backward_tiles(SPAN * c, weighted, False)
+        b0, b1, b2, b3 = (xbuf[par, b, SPAN : SPAN + 1] for b in range(4))
+        dbuf[par, reg] = b0 + b1 + b2 + b3 + fold(jnp.zeros((1, 128), jnp.float32), energy)
         dcopies = [
             remote(dbuf.at[par, reg], dbuf.at[par, reg], dsend.at[par], drecv.at[par], to_reg(k))
             for k in order
         ]
         for c in dcopies:
             c.start()
-        backward(weighted, False, rpar)
+        backward_tiles(32 - SPAN, weighted, False)
+        backward_end(rpar)
         rcopies = r_copies(rpar)
         for c in rcopies:
             c.start()
@@ -216,15 +246,18 @@
         alpha = gamma / (delta - beta * gamma / alpha_old)
         direction = own_u + beta * direction
         along = image + beta * along
+        out_ref[0:8] = solution
+        out_ref[8:16] = direction
+        out_ref[16:24] = resid[8:16]
+        out_ref[24:32] = along[8:16]
+        out_ref[32:40] = jnp.broadcast_to(alpha, (8, 128))
         solution = solution + alpha * direction
         resid = resid - alpha * along
-        for c in xcopies + rcopies + [dall]:
+        for c in sum(xcopies, []) + rcopies + [dall]:
             c.wait_send()
         return (solution, direction, resid, along, gamma, alpha)
 
-    carry = lax.fori_loop(0, ITERS, step, (zeros8, zeros8, resid0, zeros24, one, one))
-    sol_ref[...] = carry[0]
-    res_ref[...] = carry[2][8:16]
+    lax.fori_loop(0, ITERS, step, (zeros8, zeros8, resid0, zeros24, one, one))
 
 
 def solution(mesh):
@@ -233,19 +266,20 @@
 
     def body(jac_bus, pattern, branch_weight, bus_diag, right_side):
         vmem = pl.BlockSpec(memory_space=pltpu.VMEM)
-        shape = jax.ShapeDtypeStruct((8, 128), f32)
+        shape = jax.ShapeDtypeStruct((40, 128), f32)
         dma = pltpu.SemaphoreType.DMA
 
         def call(*args):
             return kernel(n_reg, n_blk, *args)
 
-        return pl.pallas_call(
+        last = pl.pallas_call(
             call,
-            out_shape=(shape, shape),
-            in_specs=[pl.BlockSpec(memory_space=pl.ANY)] + [vmem] * 4,
-            out_specs=(vmem, vmem),
+            out_shape=shape,
+            in_specs=[pl.BlockSpec(memory_space=pl.ANY)] * 5,
+            out_specs=vmem,
             scratch_shapes=[
                 pltpu.VMEM((32, 2, 128, 128), f32),
+                pltpu.VMEM((8, 8), jnp.int32),
                 pltpu.VMEM((4, 8, 128), jnp.int32),
                 pltpu.SMEM((4, 8, 128), jnp.int32),
                 pltpu.VMEM((4, 8, 128), f32),
@@ -263,12 +297,14 @@
                 pltpu.VMEM((2, 8, 128), f32),
                 pltpu.VMEM((2, 8, 128), f32),
                 pltpu.VMEM((2, 32, 1, 128), f32),
-                dma((4,)), dma, dma((2, 4)), dma((2, 4)), dma((2,)), dma((2,)),
-                dma((2, 4)), dma((2, 4)), dma((2, 4)), dma((2, 4)), dma((2,)), dma((2,)),
+                dma((4,)), dma((4,)), pltpu.SemaphoreType.REGULAR((3,)), dma, dma((2, 4)), dma((2, 4)), dma((2,)), dma((2,)),
+                dma((2, CHUNKS, 4)), dma((2, CHUNKS, 4)), dma((2, 4)), dma((2, 4)), dma((2,)), dma((2,)),
             ],
             compiler_params=pltpu.CompilerParams(collective_id=0, has_side_effects=True),
             name="pcg",
         )(jac_bus, pattern, branch_weight, bus_diag, right_side)
+        before, direction, resid, along, alpha = (last[8 * k : 8 * k + 8] for k in range(5))
+        return before + alpha * direction, resid - alpha * along
 
     axes = ("region", "blk")
     in_specs = (P("region", "blk", None, None),) + (P(axes, None),) * 4

time: 133 us -> 129 us (0.970)
  Pallas kernels: 130 us -> 127 us
  local copies, waits for them, and re-layouts: 2.53 us -> 0 us
    pallas_call x1, Pallas kernels: 130 us -> 127 us  [body(): pl.pallas_call(call, out_shape=shape, in_specs=[pl.BlockSpec(memory_space...]
    unnamed x2 -> x0, local copies, waits for them, and re-layouts: 2.53 us -> none
where the time goes in v4:
time: 129 us
  Pallas kernels  127 us (98%)
  other arithmetic  1.3 us (1%)
    pallas_call x1, Pallas kernels, body(): pl.pallas_call(call, out_shape=shape, in_specs=[pl.BlockSpec(memory_space...  127 us

profile of v4, /device:TPU:1, one launch (start us, length us, event | category | flops | bytes accessed | tf_op | source)
XLA Modules:
  0.0 129.2 jit_solution(8752334850251878071)
XLA Ops:
  0.6 127.3 %pcg.1 = f32[40,128]{1,0:T(8,128)} custom-call(f32[32,2,128,128]{3,2,1,0:T(8,128)} %args_0_.4, s32[8,8]{1,0:T(8,128)} %args_1_.4, f32[8,128]{1,0:T(8,128)} %args_2_.4, f32[8,128]{1,0:T(8,128)} %args_3_.4, f32[8,128]{1,0:T(8,128)} %args_4_.4), custom_call_target="tpu_custom_call" | custom-call | tf_op jit(solution)/shard_map/pcg/pallas_call | solution.py:275
  127.9 1.3 %multiply_subtract_fusion = (f32[8,128]{1,0:T(8,128)}, f32[8,128]{1,0:T(8,128)}) fusion(f32[40,128]{1,0:T(8,128)} %pcg.1), kind=kLoop, calls=%fused_computation | loop fusion | flops 4096 | bytes 28672 | tf_op jit(solution)/shard_map/sub | solution.py:307

commit v5 on v4

--- a/solution.py
+++ b/solution.py
@@ -6,14 +6,17 @@
 from jax.sharding import PartitionSpec as P
 
 ITERS = 12
+EARLY = 18
+EACH = 18
+INTO = 6
 CHUNKS = 2
 SPAN = 32 // CHUNKS
 MESH = pl.DeviceIdType.MESH
 
 
-def farness(k):
-    along_z, along_y = min(k // 8, 4 - k // 8), min(k // 2 % 4, 4 - k // 2 % 4)
-    return along_z + along_y
+def farness(offset):
+    steps = [min(n, 4 - n) for n in offset[:2]]
+    return (min(steps) > 0, sum(steps), offset[2] == 0)
 
 
 def kernel(
@@ -45,14 +48,14 @@
         )
 
     jcopies = [
-        pltpu.make_async_copy(jac_hbm.at[pl.ds(8 * g, 8)], jac.at[pl.ds(8 * g, 8)], jsem.at[g])
-        for g in range(4)
+        pltpu.make_async_copy(jac_hbm, jac, jsem)
+        for _ in range(1)
     ]
     icopies = [
-        pltpu.make_async_copy(pattern_hbm, pat, isem.at[0]),
-        pltpu.make_async_copy(weight_hbm, wv.at[blk], isem.at[1]),
-        pltpu.make_async_copy(diag_hbm, hsend.at[pl.ds(0, 8)], isem.at[2]),
-        pltpu.make_async_copy(rhs_hbm, hsend.at[pl.ds(8, 8)], isem.at[3]),
+        pltpu.make_async_copy(pattern_hbm, pat, isem.at[1]),
+        pltpu.make_async_copy(weight_hbm, wv.at[blk], isem.at[0]),
+        pltpu.make_async_copy(diag_hbm, hsend.at[pl.ds(0, 8)], isem.at[0]),
+        pltpu.make_async_copy(rhs_hbm, hsend.at[pl.ds(8, 8)], isem.at[0]),
     ]
     for c in icopies + jcopies:
         c.start()
@@ -67,21 +70,31 @@
             pl.semaphore_signal(far_sem.at[n], inc=1, device_id=to_reg(k), device_id_type=MESH)
 
     pv[blk] = jnp.zeros((8, 128), jnp.int32)
-    for c in icopies:
-        c.wait()
+    icopies[0].wait()
+    landed = stage.at[pl.ds(0, 24)]
+    pltpu.make_async_copy(landed, landed, isem.at[0]).wait()
     pv[blk, :, 0:8] = pat[...]
     pl.semaphore_wait(barrier, len(near))
 
     gcopies = []
     for k in range(1, n_blk):
-        gcopies.append(remote(pv.at[blk], pv.at[blk], gsend.at[0, k], grecv.at[0, k], to_blk(k)))
-        gcopies.append(remote(wv.at[blk], wv.at[blk], gsend.at[1, k], grecv.at[1, k], to_blk(k)))
+        gcopies.append(remote(pv.at[blk], pv.at[blk], gsend.at[0], grecv.at[0], to_blk(k)))
+        gcopies.append(remote(wv.at[blk], wv.at[blk], gsend.at[1], grecv.at[1], to_blk(k)))
     hcopies = [
-        remote(hsend, hbuf.at[0], hsend_sem.at[0], hrecv.at[0], to_reg(1)),
-        remote(hsend, hbuf.at[1], hsend_sem.at[1], hrecv.at[1], to_reg(-1)),
+        remote(hsend, hbuf.at[0], hsend_sem, hrecv, to_reg(1)),
+        remote(hsend, hbuf.at[1], hsend_sem, hrecv, to_reg(-1)),
     ]
     for c in gcopies + hcopies:
         c.start()
+
+    def whole(ref, ssem, rsem):
+        return remote(ref, ref, ssem, rsem, to_blk(1))
+
+    gcopies = [
+        whole(pv.at[pl.ds(0, n_blk - 1)], gsend.at[0], grecv.at[0]),
+        whole(wv.at[pl.ds(0, n_blk - 1)], gsend.at[1], grecv.at[1]),
+    ]
+    hcopies = [whole(hbuf, hsend_sem, hrecv)]
     far_signal(0)
     pl.semaphore_wait(far_sem.at[0], 2)
     far_signal(1)
@@ -90,7 +103,6 @@
     pcopy = pltpu.make_async_copy(pv, psm, psem)
     pcopy.start()
 
-    lane = lax.broadcasted_iota(jnp.int32, (1, 128), 1)
     patf = pv[...].astype(jnp.float32).reshape(32, 128)
     lanes32 = lax.broadcasted_iota(jnp.int32, (32, 128), 1)
     for j in range(2):
@@ -115,8 +127,10 @@
             total = total + part[slot, pl.ds(k, 8, stride=8), :]
         return total
 
-    def backward_tiles(first, rows, square):
+    def backward_tiles(first, rows, square, beside=()):
         for t in range(first, first + rows.shape[0]):
+            for copy in beside[EACH * (t - first) : EACH * (t - first) + EACH]:
+                copy.start()
             wc = jnp.broadcast_to(rows[t - first : t - first + 1], (128, 128)).T
             for j in range(2):
                 tile = jac[t, j]
@@ -137,11 +151,14 @@
 
     def r_copies(par):
         return [
-            remote(csend.at[par, pl.ds(16, 8)], rlo8.at[par], rsend.at[par, 0], rrecv.at[par, 0], to_reg(2)),
-            remote(csend.at[par, pl.ds(0, 8)], rhi8.at[par], rsend.at[par, 1], rrecv.at[par, 1], to_reg(-2)),
-            remote(csend.at[par, pl.ds(8, 16)], rlo16.at[par], rsend.at[par, 2], rrecv.at[par, 2], to_reg(1)),
-            remote(csend.at[par, pl.ds(0, 16)], rhi16.at[par], rsend.at[par, 3], rrecv.at[par, 3], to_reg(-1)),
+            remote(csend.at[par, pl.ds(16, 8)], rlo8.at[par], rsend.at[par], rrecv.at[par], to_reg(2)),
+            remote(csend.at[par, pl.ds(0, 8)], rhi8.at[par], rsend.at[par], rrecv.at[par], to_reg(-2)),
+            remote(csend.at[par, pl.ds(8, 16)], rlo16.at[par], rsend.at[par], rrecv.at[par], to_reg(1)),
+            remote(csend.at[par, pl.ds(0, 16)], rhi16.at[par], rsend.at[par], rrecv.at[par], to_reg(-1)),
         ]
+
+    def r_whole(par):
+        return whole(xbuf.at[par, pl.ds(0, 2), pl.ds(0, 24)], rsend.at[par], rrecv.at[par])
 
     def r_sum(par):
         before = rlo8[par] + rlo16[par, 0:8] + csend[par, 0:8]
@@ -161,8 +178,8 @@
     pcopy.wait()
     for c in hcopies:
         c.wait_recv()
-    for c in copies:
-        c.wait_recv()
+    copies = [r_whole(0)]
+    copies[0].wait_recv()
     diag[...] = jnp.concatenate([hbuf[0, 0:8], hsend[0:8], hbuf[1, 0:8]], axis=0)
     resid0 = jnp.concatenate([hbuf[0, 8:16], hsend[8:16], hbuf[1, 8:16]], axis=0)
     inv = 1.0 / (diag[...] + r_sum(0))
@@ -170,18 +187,21 @@
         c.wait_send()
     pl.semaphore_wait(far_sem.at[2], 2)
 
-    order = sorted(range(1, n_reg), key=farness, reverse=True)
+    offsets = [(z, y, c) for z in range(n_reg // 8) for y in range(4) for c in range(2)][1:]
+    order = sorted(offsets, key=farness, reverse=True)
+
+    def to_offset(offset):
+        z, y, c = offset
+        there_z = lax.rem(reg // 8 + z, n_reg // 8)
+        there_y = lax.rem(lax.rem(reg // 2, 4) + y, 4)
+        return ((there_z * 4 + there_y) * 2 + lax.rem(reg + c, 2), blk)
+
     zeros8 = jnp.zeros((8, 128), jnp.float32)
     zeros24 = jnp.zeros((24, 128), jnp.float32)
-    one = jnp.ones((1, 1), jnp.float32)
-
-    def fold(first, second):
-        both = jnp.where(lane < 64, first, second)
-        rest = jnp.where(lane < 64, second, first)
-        return both + pltpu.roll(rest, 64, 1)
+    none = jnp.zeros((1, 1), jnp.float32)
 
     def step(i, carry):
-        solution, direction, resid, along, gamma_old, alpha_old = carry
+        solution, direction, resid, along, over_gamma, over_alpha = carry
         par = lax.rem(i, 2)
         rpar = lax.rem(i + 1, 2)
         scaled = inv * resid
@@ -189,11 +209,15 @@
         own_u = scaled[8:16]
         first = jnp.sum(own_u * resid[8:16], axis=0, keepdims=True)
         second = jnp.sum(own_u * own_u * diag[8:16], axis=0, keepdims=True)
-        xbuf[par, blk, SPAN : SPAN + 1] = fold(first, second)
+        xbuf[par, blk, SPAN : SPAN + 1] = first
+        xbuf[par, blk, SPAN + 1 : SPAN + 2] = second
 
         xcopies = []
         for c in range(CHUNKS):
             for t in range(SPAN * c, SPAN * c + SPAN):
+                if c and t == SPAN * c + INTO:
+                    for copy in xcopies[c - 1]:
+                        copy.start()
                 x0 = uv[pl.ds(psm[t // 8, t % 8, 2 * blk], 1), :]
                 x1 = uv[pl.ds(psm[t // 8, t % 8, 2 * blk + 1], 1), :]
                 both = jac[t, 0] * x0 + jac[t, 1] * x1
@@ -201,49 +225,46 @@
             at = SPAN * c + (8 if c else 0)
             for g in range(SPAN // 8):
                 xbuf[par, blk, at + 8 * g : at + 8 * g + 8] = group_rows(SPAN // 8 * c + g)
-            mine = xbuf.at[par, blk, pl.ds(at, SPAN if c else SPAN + 1)]
+            mine = xbuf.at[par, blk, pl.ds(at, SPAN if c else SPAN + 2)]
             xcopies.append([
-                remote(mine, mine, xsend.at[par, c, k], xrecv.at[par, c, k], to_blk(k))
+                remote(mine, mine, xsend.at[par], xrecv.at[par, c], to_blk(k))
                 for k in (2, 1, 3)
             ])
-            for copy in xcopies[c]:
-                copy.start()
+        for copy in xcopies[-1]:
+            copy.start()
         energy = jnp.zeros((1, 128), jnp.float32)
         for c in range(CHUNKS):
-            for copy in xcopies[c]:
-                copy.wait_recv()
             at = SPAN * c + (8 if c else 0)
+            landed = xbuf.at[par, pl.ds(0, n_blk - 1), pl.ds(at, SPAN if c else SPAN + 2)]
+            whole(landed, xsend.at[par], xrecv.at[par, c]).wait_recv()
             b0, b1, b2, b3 = (xbuf[par, b, at : at + SPAN] for b in range(4))
             rows = b0 + b1 + b2 + b3
             weighted = weight[SPAN * c : SPAN * c + SPAN] * rows
             energy = energy + jnp.sum(weighted * rows, axis=0, keepdims=True)
             if c < CHUNKS - 1:
                 backward_tiles(SPAN * c, weighted, False)
-        b0, b1, b2, b3 = (xbuf[par, b, SPAN : SPAN + 1] for b in range(4))
-        dbuf[par, reg] = b0 + b1 + b2 + b3 + fold(jnp.zeros((1, 128), jnp.float32), energy)
+        b0, b1, b2, b3 = (xbuf[par, b, SPAN : SPAN + 2] for b in range(4))
+        row = lax.broadcasted_iota(jnp.int32, (2, 128), 0)
+        dbuf[par, reg] = b0 + b1 + b2 + b3 + jnp.where(row == 1, energy, 0.0)
         dcopies = [
-            remote(dbuf.at[par, reg], dbuf.at[par, reg], dsend.at[par], drecv.at[par], to_reg(k))
+            remote(dbuf.at[par, reg], dbuf.at[par, reg], dsend.at[par], drecv.at[par], to_offset(k))
             for k in order
         ]
-        for c in dcopies:
-            c.start()
-        backward_tiles(32 - SPAN, weighted, False)
+        backward_tiles(32 - SPAN, weighted, False, dcopies[:EARLY])
         backward_end(rpar)
         rcopies = r_copies(rpar)
-        for c in rcopies:
+        for c in rcopies + dcopies[EARLY:]:
             c.start()
-        for c in rcopies:
-            c.wait_recv()
+        rall = r_whole(rpar)
+        rall.wait_recv()
         image = diag[...] * scaled + r_sum(rpar)
         others = dbuf.at[par, pl.ds(0, n_reg - 1)]
         dall = remote(others, others, dsend.at[par], drecv.at[par], to_reg(1))
         dall.wait_recv()
-        sums = jnp.sum(dbuf[par].reshape(n_reg, 128), axis=0, keepdims=True)
-        gamma = jnp.sum(jnp.where(lane < 64, sums, 0.0), axis=1, keepdims=True)
-        delta = jnp.sum(jnp.where(lane < 64, 0.0, sums), axis=1, keepdims=True)
-        begun = jnp.where(i == 0, 0.0, 1.0)
-        beta = begun * gamma / gamma_old
-        alpha = gamma / (delta - beta * gamma / alpha_old)
+        sums = jnp.sum(jnp.sum(dbuf[par], axis=0), axis=1, keepdims=True)
+        gamma, delta = sums[0:1], sums[1:2]
+        beta = gamma * over_gamma
+        alpha = gamma / (delta - beta * gamma * over_alpha)
         direction = own_u + beta * direction
         along = image + beta * along
         out_ref[0:8] = solution
@@ -253,11 +274,13 @@
         out_ref[32:40] = jnp.broadcast_to(alpha, (8, 128))
         solution = solution + alpha * direction
         resid = resid - alpha * along
-        for c in sum(xcopies, []) + rcopies + [dall]:
+        sent = xbuf.at[par, pl.ds(0, n_blk - 1), pl.ds(0, 34)]
+        xall = whole(sent, xsend.at[par], xrecv.at[par, 0])
+        for c in (xall, rall, dall):
             c.wait_send()
-        return (solution, direction, resid, along, gamma, alpha)
-
-    lax.fori_loop(0, ITERS, step, (zeros8, zeros8, resid0, zeros24, one, one))
+        return (solution, direction, resid, along, 1.0 / gamma, 1.0 / alpha)
+
+    lax.fori_loop(0, ITERS, step, (zeros8, zeros8, resid0, zeros24, none, none))
 
 
 def solution(mesh):
@@ -296,9 +319,9 @@
                 pltpu.VMEM((2, 16, 128), f32),
                 pltpu.VMEM((2, 8, 128), f32),
                 pltpu.VMEM((2, 8, 128), f32),
-                pltpu.VMEM((2, 32, 1, 128), f32),
-                dma((4,)), dma((4,)), pltpu.SemaphoreType.REGULAR((3,)), dma, dma((2, 4)), dma((2, 4)), dma((2,)), dma((2,)),
-                dma((2, CHUNKS, 4)), dma((2, CHUNKS, 4)), dma((2, 4)), dma((2, 4)), dma((2,)), dma((2,)),
+                pltpu.VMEM((2, 32, 2, 128), f32),
+                dma, dma((2,)), pltpu.SemaphoreType.REGULAR((3,)), dma, dma((2,)), dma((2,)), dma, dma,
+                dma((2,)), dma((2, CHUNKS)), dma((2,)), dma((2,)), dma((2,)), dma((2,)),
             ],
             compiler_params=pltpu.CompilerParams(collective_id=0, has_side_effects=True),
             name="pcg",

time: 129 us -> 129 us (level)
  no operation moved by 1% of the time
where the time goes in v5:
time: 129 us
  Pallas kernels  127 us (98%)
  other arithmetic  1.3 us (1%)
    pallas_call x1, Pallas kernels, body(): pl.pallas_call(call, out_shape=shape, in_specs=[pl.BlockSpec(memory_space...  127 us

profile of v5, /device:TPU:1, one launch (start us, length us, event | category | flops | bytes accessed | tf_op | source)
XLA Modules:
  0.0 128.8 jit_solution(447342645460858399)
XLA Ops:
  0.6 126.9 %pcg.1 = f32[40,128]{1,0:T(8,128)} custom-call(f32[32,2,128,128]{3,2,1,0:T(8,128)} %args_0_.4, s32[8,8]{1,0:T(8,128)} %args_1_.4, f32[8,128]{1,0:T(8,128)} %args_2_.4, f32[8,128]{1,0:T(8,128)} %args_3_.4, f32[8,128]{1,0:T(8,128)} %args_4_.4), custom_call_target="tpu_custom_call" | custom-call | tf_op jit(solution)/shard_map/pcg/pallas_call | solution.py:298
  127.5 1.3 %multiply_subtract_fusion = (f32[8,128]{1,0:T(8,128)}, f32[8,128]{1,0:T(8,128)}) fusion(f32[40,128]{1,0:T(8,128)} %pcg.1), kind=kLoop, calls=%fused_computation | loop fusion | flops 4096 | bytes 28672 | tf_op jit(solution)/shard_map/sub | solution.py:330

commit v6 on v5

--- a/solution.py
+++ b/solution.py
@@ -8,7 +8,7 @@
 ITERS = 12
 EARLY = 18
 EACH = 18
-INTO = 6
+INTO = 1
 CHUNKS = 2
 SPAN = 32 // CHUNKS
 MESH = pl.DeviceIdType.MESH
@@ -23,7 +23,7 @@
     n_reg, n_blk,
     jac_hbm, pattern_hbm, weight_hbm, diag_hbm, rhs_hbm,
     out_ref,
-    jac, pat, pv, psm, wv, hsend, hbuf, oht, stage, part, uv, diag, xbuf, csend, rlo16, rhi16, rlo8, rhi8, dbuf,
+    jac, pat, pv, psm, wv, hsend, hbuf, oht, stage, part, uv, qv, diag, xbuf, csend, rlo16, rhi16, rlo8, rhi8, dbuf,
     jsem, isem, far_sem, psem, gsend, grecv, hsend_sem, hrecv, xsend, xrecv, rsend, rrecv, dsend, drecv,
 ):
     reg = lax.axis_index("region")
@@ -200,41 +200,35 @@
     zeros24 = jnp.zeros((24, 128), jnp.float32)
     none = jnp.zeros((1, 1), jnp.float32)
 
-    def step(i, carry):
-        solution, direction, resid, along, over_gamma, over_alpha = carry
-        par = lax.rem(i, 2)
-        rpar = lax.rem(i + 1, 2)
-        scaled = inv * resid
-        uv[...] = scaled
-        own_u = scaled[8:16]
-        first = jnp.sum(own_u * resid[8:16], axis=0, keepdims=True)
+    def forward_tiles(source_ref, c, before=()):
+        for t in range(SPAN * c, SPAN * c + SPAN):
+            if t == SPAN * c + INTO:
+                for copy in before:
+                    copy.start()
+            x0 = source_ref[pl.ds(psm[t // 8, t % 8, 2 * blk], 1), :]
+            x1 = source_ref[pl.ds(psm[t // 8, t % 8, 2 * blk + 1], 1), :]
+            both = jac[t, 0] * x0 + jac[t, 1] * x1
+            part[t // 8, 8 * (t % 8) : 8 * (t % 8) + 8] = eight_sums(both.T)
+        return jnp.concatenate([group_rows(SPAN // 8 * c + g) for g in range(SPAN // 8)], axis=0)
+
+    def chunk_at(c):
+        return SPAN * c + (8 if c else 0)
+
+    def place(par, c, rows):
+        xbuf[par, blk, chunk_at(c) : chunk_at(c) + SPAN] = rows
+        mine = xbuf.at[par, blk, pl.ds(chunk_at(c), SPAN if c else SPAN + 2)]
+        return [remote(mine, mine, xsend.at[par], xrecv.at[par, c], to_blk(k)) for k in (2, 1, 3)]
+
+    def place_sums(par, own_u, own_r):
+        first = jnp.sum(own_u * own_r, axis=0, keepdims=True)
         second = jnp.sum(own_u * own_u * diag[8:16], axis=0, keepdims=True)
         xbuf[par, blk, SPAN : SPAN + 1] = first
         xbuf[par, blk, SPAN + 1 : SPAN + 2] = second
 
-        xcopies = []
-        for c in range(CHUNKS):
-            for t in range(SPAN * c, SPAN * c + SPAN):
-                if c and t == SPAN * c + INTO:
-                    for copy in xcopies[c - 1]:
-                        copy.start()
-                x0 = uv[pl.ds(psm[t // 8, t % 8, 2 * blk], 1), :]
-                x1 = uv[pl.ds(psm[t // 8, t % 8, 2 * blk + 1], 1), :]
-                both = jac[t, 0] * x0 + jac[t, 1] * x1
-                part[t // 8, 8 * (t % 8) : 8 * (t % 8) + 8] = eight_sums(both.T)
-            at = SPAN * c + (8 if c else 0)
-            for g in range(SPAN // 8):
-                xbuf[par, blk, at + 8 * g : at + 8 * g + 8] = group_rows(SPAN // 8 * c + g)
-            mine = xbuf.at[par, blk, pl.ds(at, SPAN if c else SPAN + 2)]
-            xcopies.append([
-                remote(mine, mine, xsend.at[par], xrecv.at[par, c], to_blk(k))
-                for k in (2, 1, 3)
-            ])
-        for copy in xcopies[-1]:
-            copy.start()
+    def bus_sums(par, rpar, wide):
         energy = jnp.zeros((1, 128), jnp.float32)
         for c in range(CHUNKS):
-            at = SPAN * c + (8 if c else 0)
+            at = chunk_at(c)
             landed = xbuf.at[par, pl.ds(0, n_blk - 1), pl.ds(at, SPAN if c else SPAN + 2)]
             whole(landed, xsend.at[par], xrecv.at[par, c]).wait_recv()
             b0, b1, b2, b3 = (xbuf[par, b, at : at + SPAN] for b in range(4))
@@ -252,35 +246,77 @@
         ]
         backward_tiles(32 - SPAN, weighted, False, dcopies[:EARLY])
         backward_end(rpar)
-        rcopies = r_copies(rpar)
-        for c in rcopies + dcopies[EARLY:]:
+        for c in r_copies(rpar)[0 if wide else 2 :] + dcopies[EARLY:]:
             c.start()
-        rall = r_whole(rpar)
-        rall.wait_recv()
-        image = diag[...] * scaled + r_sum(rpar)
         others = dbuf.at[par, pl.ds(0, n_reg - 1)]
-        dall = remote(others, others, dsend.at[par], drecv.at[par], to_reg(1))
-        dall.wait_recv()
+        return whole(others, dsend.at[par], drecv.at[par])
+
+    def scalars(par, over_gamma, over_alpha):
         sums = jnp.sum(jnp.sum(dbuf[par], axis=0), axis=1, keepdims=True)
         gamma, delta = sums[0:1], sums[1:2]
         beta = gamma * over_gamma
         alpha = gamma / (delta - beta * gamma * over_alpha)
-        direction = own_u + beta * direction
+        return gamma, alpha, beta
+
+    def sent_whole(par):
+        sent = xbuf.at[par, pl.ds(0, n_blk - 1), pl.ds(0, 34)]
+        return whole(sent, xsend.at[par], xrecv.at[par, 0])
+
+    uv[...] = inv * resid0
+    place_sums(0, uv[8:16], resid0[8:16])
+    for c in range(CHUNKS):
+        for copy in place(0, c, forward_tiles(uv, c)):
+            copy.start()
+
+    def step(i, carry):
+        solution, direction, resid, along, over_gamma, over_alpha = carry
+        par = lax.rem(i, 2)
+        rpar = lax.rem(i + 1, 2)
+        scaled = inv * resid
+        uv[...] = scaled
+        qv[...] = inv * along
+        dall = bus_sums(par, rpar, True)
+        kept_u = [forward_tiles(uv, c) for c in range(CHUNKS)]
+        kept_q = [forward_tiles(qv, c) for c in range(CHUNKS)]
+        rall = r_whole(rpar)
+        rall.wait_recv()
+        image = diag[...] * scaled + r_sum(rpar)
+        uv[...] = inv * image
+        fresh = forward_tiles(uv, 0)
+        dall.wait_recv()
+        gamma, alpha, beta = scalars(par, over_gamma, over_alpha)
+        direction = scaled[8:16] + beta * direction
         along = image + beta * along
-        out_ref[0:8] = solution
-        out_ref[8:16] = direction
-        out_ref[16:24] = resid[8:16]
-        out_ref[24:32] = along[8:16]
-        out_ref[32:40] = jnp.broadcast_to(alpha, (8, 128))
         solution = solution + alpha * direction
         resid = resid - alpha * along
-        sent = xbuf.at[par, pl.ds(0, n_blk - 1), pl.ds(0, 34)]
-        xall = whole(sent, xsend.at[par], xrecv.at[par, 0])
-        for c in (xall, rall, dall):
+        place_sums(rpar, inv[8:16] * resid[8:16], resid[8:16])
+        copies = place(rpar, 0, kept_u[0] - alpha * (fresh + beta * kept_q[0]))
+        for c in range(1, CHUNKS):
+            fresh = forward_tiles(uv, c, copies)
+            copies = place(rpar, c, kept_u[c] - alpha * (fresh + beta * kept_q[c]))
+        for copy in copies:
+            copy.start()
+        for c in (sent_whole(par), rall, dall):
             c.wait_send()
         return (solution, direction, resid, along, 1.0 / gamma, 1.0 / alpha)
 
-    lax.fori_loop(0, ITERS, step, (zeros8, zeros8, resid0, zeros24, none, none))
+    carry = lax.fori_loop(0, ITERS - 1, step, (zeros8, zeros8, resid0, zeros24, none, none))
+    solution, direction, resid, along, over_gamma, over_alpha = carry
+    par, rpar = (ITERS - 1) % 2, ITERS % 2
+    dall = bus_sums(par, rpar, False)
+    rall = whole(xbuf.at[rpar, pl.ds(0, 2), pl.ds(0, 16)], rsend.at[rpar], rrecv.at[rpar])
+    rall.wait_recv()
+    scaled = inv[8:16] * resid[8:16]
+    image = diag[8:16] * scaled + (rlo16[rpar, 8:16] + csend[rpar, 8:16] + rhi16[rpar, 0:8])
+    dall.wait_recv()
+    gamma, alpha, beta = scalars(par, over_gamma, over_alpha)
+    out_ref[0:8] = solution
+    out_ref[8:16] = scaled + beta * direction
+    out_ref[16:24] = resid[8:16]
+    out_ref[24:32] = image + beta * along[8:16]
+    out_ref[32:40] = jnp.broadcast_to(alpha, (8, 128))
+    for c in (sent_whole(par), rall, dall):
+        c.wait_send()
 
 
 def solution(mesh):
@@ -313,6 +349,7 @@
                 pltpu.VMEM((8, 64, 128), f32),
                 pltpu.VMEM((24, 128), f32),
                 pltpu.VMEM((24, 128), f32),
+                pltpu.VMEM((24, 128), f32),
                 pltpu.VMEM((2, 4, 40, 128), f32),
                 pltpu.VMEM((2, 24, 128), f32),
                 pltpu.VMEM((2, 16, 128), f32),

time: 129 us -> 128 us (level)
  no operation moved by 1% of the time
where the time goes in v6:
time: 128 us
  Pallas kernels  126 us (98%)
  other arithmetic  1.3 us (1%)
    pallas_call x1, Pallas kernels, body(): pl.pallas_call(call, out_shape=shape, in_specs=[pl.BlockSpec(memory_space...  126 us

profile of v6, /device:TPU:1, one launch (start us, length us, event | category | flops | bytes accessed | tf_op | source)
XLA Modules:
  0.0 127.6 jit_solution(4957744965251342787)
XLA Ops:
  0.6 125.7 %pcg.1 = f32[40,128]{1,0:T(8,128)} custom-call(f32[32,2,128,128]{3,2,1,0:T(8,128)} %args_0_.4, s32[8,8]{1,0:T(8,128)} %args_1_.4, f32[8,128]{1,0:T(8,128)} %args_2_.4, f32[8,128]{1,0:T(8,128)} %args_3_.4, f32[8,128]{1,0:T(8,128)} %args_4_.4), custom_call_target="tpu_custom_call" | custom-call | tf_op jit(solution)/shard_map/pcg/pallas_call | solution.py:334
  126.3 1.3 %multiply_subtract_fusion = (f32[8,128]{1,0:T(8,128)}, f32[8,128]{1,0:T(8,128)}) fusion(f32[40,128]{1,0:T(8,128)} %pcg.1), kind=kLoop, calls=%fused_computation | loop fusion | flops 4096 | bytes 28672 | tf_op jit(solution)/shard_map/sub | solution.py:367

commit v7 on v6

--- a/solution.py
+++ b/solution.py
@@ -7,7 +7,7 @@
 
 ITERS = 12
 EARLY = 18
-EACH = 18
+EACH = 5
 INTO = 1
 CHUNKS = 2
 SPAN = 32 // CHUNKS
@@ -227,19 +227,22 @@
 
     def bus_sums(par, rpar, wide):
         energy = jnp.zeros((1, 128), jnp.float32)
+        low_lanes = lax.broadcasted_iota(jnp.int32, (1, 128), 1) < 64
         for c in range(CHUNKS):
             at = chunk_at(c)
             landed = xbuf.at[par, pl.ds(0, n_blk - 1), pl.ds(at, SPAN if c else SPAN + 2)]
             whole(landed, xsend.at[par], xrecv.at[par, c]).wait_recv()
-            b0, b1, b2, b3 = (xbuf[par, b, at : at + SPAN] for b in range(4))
-            rows = b0 + b1 + b2 + b3
+            b0, b1, b2, b3 = (xbuf[par, b, at : at + (SPAN if c else SPAN + 2)] for b in range(4))
+            rows = b0[:SPAN] + b1[:SPAN] + b2[:SPAN] + b3[:SPAN]
             weighted = weight[SPAN * c : SPAN * c + SPAN] * rows
             energy = energy + jnp.sum(weighted * rows, axis=0, keepdims=True)
+            if c == 0:
+                first = b0[SPAN:] + b1[SPAN:] + b2[SPAN:] + b3[SPAN:]
+                first = first + pltpu.roll(first, 64, 1)
+                held = jnp.where(low_lanes, first[0:1], first[1:2])
             if c < CHUNKS - 1:
                 backward_tiles(SPAN * c, weighted, False)
-        b0, b1, b2, b3 = (xbuf[par, b, SPAN : SPAN + 2] for b in range(4))
-        row = lax.broadcasted_iota(jnp.int32, (2, 128), 0)
-        dbuf[par, reg] = b0 + b1 + b2 + b3 + jnp.where(row == 1, energy, 0.0)
+        dbuf[par, reg] = held + jnp.where(low_lanes, 0.0, energy + pltpu.roll(energy, 64, 1))
         dcopies = [
             remote(dbuf.at[par, reg], dbuf.at[par, reg], dsend.at[par], drecv.at[par], to_offset(k))
             for k in order
@@ -252,8 +255,10 @@
         return whole(others, dsend.at[par], drecv.at[par])
 
     def scalars(par, over_gamma, over_alpha):
-        sums = jnp.sum(jnp.sum(dbuf[par], axis=0), axis=1, keepdims=True)
-        gamma, delta = sums[0:1], sums[1:2]
+        sums = jnp.sum(dbuf[par], axis=0)
+        low_lanes = lax.broadcasted_iota(jnp.int32, (1, 128), 1) < 64
+        gamma = jnp.sum(jnp.where(low_lanes, sums, 0.0), axis=1, keepdims=True)
+        delta = jnp.sum(jnp.where(low_lanes, 0.0, sums), axis=1, keepdims=True)
         beta = gamma * over_gamma
         alpha = gamma / (delta - beta * gamma * over_alpha)
         return gamma, alpha, beta
@@ -356,7 +361,7 @@
                 pltpu.VMEM((2, 16, 128), f32),
                 pltpu.VMEM((2, 8, 128), f32),
                 pltpu.VMEM((2, 8, 128), f32),
-                pltpu.VMEM((2, 32, 2, 128), f32),
+                pltpu.VMEM((2, 32, 1, 128), f32),
                 dma, dma((2,)), pltpu.SemaphoreType.REGULAR((3,)), dma, dma((2,)), dma((2,)), dma, dma,
                 dma((2,)), dma((2, CHUNKS)), dma((2,)), dma((2,)), dma((2,)), dma((2,)),
             ],

time: 128 us -> 128 us (level)
  no operation moved by 1% of the time
where the time goes in v7:
time: 128 us
  Pallas kernels  126 us (98%)
  other arithmetic  1.3 us (1%)
    pallas_call x1, Pallas kernels, body(): pl.pallas_call(call, out_shape=shape, in_specs=[pl.BlockSpec(memory_space...  126 us

profile of v7, /device:TPU:1, one launch (start us, length us, event | category | flops | bytes accessed | tf_op | source)
XLA Modules:
  0.0 127.6 jit_solution(14152225970370215367)
XLA Ops:
  0.6 125.7 %pcg.1 = f32[40,128]{1,0:T(8,128)} custom-call(f32[32,2,128,128]{3,2,1,0:T(8,128)} %args_0_.4, s32[8,8]{1,0:T(8,128)} %args_1_.4, f32[8,128]{1,0:T(8,128)} %args_2_.4, f32[8,128]{1,0:T(8,128)} %args_3_.4, f32[8,128]{1,0:T(8,128)} %args_4_.4), custom_call_target="tpu_custom_call" | custom-call | tf_op jit(solution)/shard_map/pcg/pallas_call | solution.py:339
  126.3 1.3 %multiply_subtract_fusion = (f32[8,128]{1,0:T(8,128)}, f32[8,128]{1,0:T(8,128)}) fusion(f32[40,128]{1,0:T(8,128)} %pcg.1), kind=kLoop, calls=%fused_computation | loop fusion | flops 4096 | bytes 28672 | tf_op jit(solution)/shard_map/sub | solution.py:372

commit v8 on v7

--- a/solution.py
+++ b/solution.py
@@ -267,7 +267,9 @@
         sent = xbuf.at[par, pl.ds(0, n_blk - 1), pl.ds(0, 34)]
         return whole(sent, xsend.at[par], xrecv.at[par, 0])
 
-    uv[...] = inv * resid0
+    uv[0:24] = inv * resid0
+    uv[24:32] = zeros8
+    qv[24:32] = zeros8
     place_sums(0, uv[8:16], resid0[8:16])
     for c in range(CHUNKS):
         for copy in place(0, c, forward_tiles(uv, c)):
@@ -278,15 +280,15 @@
         par = lax.rem(i, 2)
         rpar = lax.rem(i + 1, 2)
         scaled = inv * resid
-        uv[...] = scaled
-        qv[...] = inv * along
+        uv[0:24] = scaled
+        qv[0:24] = inv * along
         dall = bus_sums(par, rpar, True)
         kept_u = [forward_tiles(uv, c) for c in range(CHUNKS)]
         kept_q = [forward_tiles(qv, c) for c in range(CHUNKS)]
         rall = r_whole(rpar)
         rall.wait_recv()
         image = diag[...] * scaled + r_sum(rpar)
-        uv[...] = inv * image
+        uv[0:24] = inv * image
         fresh = forward_tiles(uv, 0)
         dall.wait_recv()
         gamma, alpha, beta = scalars(par, over_gamma, over_alpha)
@@ -351,9 +353,9 @@
                 pltpu.VMEM((2, 16, 128), f32),
                 pltpu.VMEM((32, 256), jnp.bfloat16),
                 pltpu.VMEM((128, 128), f32),
-                pltpu.VMEM((8, 64, 128), f32),
-                pltpu.VMEM((24, 128), f32),
-                pltpu.VMEM((24, 128), f32),
+                pltpu.VMEM((8, 72, 128), f32),
+                pltpu.VMEM((32, 128), f32),
+                pltpu.VMEM((32, 128), f32),
                 pltpu.VMEM((24, 128), f32),
                 pltpu.VMEM((2, 4, 40, 128), f32),
                 pltpu.VMEM((2, 24, 128), f32),

time: 128 us -> 128 us (level)
  no operation moved by 1% of the time
where the time goes in v8:
time: 128 us
  Pallas kernels  126 us (98%)
  other arithmetic  1.3 us (1%)
    pallas_call x1, Pallas kernels, body(): pl.pallas_call(call, out_shape=shape, in_specs=[pl.BlockSpec(memory_space...  126 us

profile of v8, /device:TPU:1, one launch (start us, length us, event | category | flops | bytes accessed | tf_op | source)
XLA Modules:
  0.0 127.6 jit_solution(6602520761503948288)
XLA Ops:
  0.6 125.6 %pcg.1 = f32[40,128]{1,0:T(8,128)} custom-call(f32[32,2,128,128]{3,2,1,0:T(8,128)} %args_0_.4, s32[8,8]{1,0:T(8,128)} %args_1_.4, f32[8,128]{1,0:T(8,128)} %args_2_.4, f32[8,128]{1,0:T(8,128)} %args_3_.4, f32[8,128]{1,0:T(8,128)} %args_4_.4), custom_call_target="tpu_custom_call" | custom-call | tf_op jit(solution)/shard_map/pcg/pallas_call | solution.py:341
  126.3 1.3 %multiply_subtract_fusion = (f32[8,128]{1,0:T(8,128)}, f32[8,128]{1,0:T(8,128)}) fusion(f32[40,128]{1,0:T(8,128)} %pcg.1), kind=kLoop, calls=%fused_computation | loop fusion | flops 4096 | bytes 28672 | tf_op jit(solution)/shard_map/sub | solution.py:374

commit v9 on v8

--- a/solution.py
+++ b/solution.py
@@ -142,11 +142,9 @@
     def backward_end(par):
         whole = jnp.concatenate([group_rows(k) for k in range(8)], axis=0)
         high = whole.astype(jnp.bfloat16)
-        rest = whole - high.astype(jnp.float32)
-        mid = rest.astype(jnp.bfloat16)
-        low = (rest - mid.astype(jnp.float32)).astype(jnp.bfloat16)
-        stack = jnp.concatenate([high, mid, low, jnp.zeros((64, 128), jnp.bfloat16)], axis=0)
-        total = jnp.dot(oht[...], stack, preferred_element_type=jnp.float32)
+        mid = (whole - high.astype(jnp.float32)).astype(jnp.bfloat16)
+        stack = jnp.concatenate([high, mid], axis=0)
+        total = jnp.dot(oht[:, 0:128], stack, preferred_element_type=jnp.float32)
         csend[par] = total[0:24]
 
     def r_copies(par):

time: 128 us -> 128 us (level)
  no operation moved by 1% of the time
where the time goes in v9:
time: 128 us; the launch traced here: 127 us
  Pallas kernels  126 us (98%)
  other arithmetic  1.3 us (1%)
    pallas_call x1, Pallas kernels, body(): pl.pallas_call(call, out_shape=shape, in_specs=[pl.BlockSpec(memory_space...  126 us

profile of v9, /device:TPU:1, one launch (start us, length us, event | category | flops | bytes accessed | tf_op | source)
XLA Modules:
  0.0 127.5 jit_solution(1855420491055973847)
XLA Ops:
  0.6 125.5 %pcg.1 = f32[40,128]{1,0:T(8,128)} custom-call(f32[32,2,128,128]{3,2,1,0:T(8,128)} %args_0_.4, s32[8,8]{1,0:T(8,128)} %args_1_.4, f32[8,128]{1,0:T(8,128)} %args_2_.4, f32[8,128]{1,0:T(8,128)} %args_3_.4, f32[8,128]{1,0:T(8,128)} %args_4_.4), custom_call_target="tpu_custom_call" | custom-call | tf_op jit(solution)/shard_map/pcg/pallas_call | solution.py:339
  126.2 1.3 %multiply_subtract_fusion = (f32[8,128]{1,0:T(8,128)}, f32[8,128]{1,0:T(8,128)}) fusion(f32[40,128]{1,0:T(8,128)} %pcg.1), kind=kLoop, calls=%fused_computation | loop fusion | flops 4096 | bytes 28672 | tf_op jit(solution)/shard_map/sub | solution.py:372
